TPU v7x, 32 devices: a whole 2x2x4 slice. The times are simulated.
32 devices in a mesh: dp: 16 (over z, x, core), tp: 2 (over y).
Axes of the slice: x: 2, y: 2, z: 4, core: 2. Of those that a mesh axis runs over, the one named last changes fastest.
Arguments:
- inputs: bfloat16 [32768, 640], P('dp'), may hold values from -6 to 6
- out_grad: bfloat16 [32768, 640], P('dp'), may hold values from -6 to 6
- segment_ids: int32 [32, 1024], P('dp'), may hold values from 0 to 5, never falling along the last dimension, each value on 1 to 400 neighbouring positions
- attn_weights: float32 [4, 640, 640], P(None, 'dp', 'tp'), may hold values from -6 to 6
- ffn_weights: float32 [2, 640, 2560], P(None, 'dp', 'tp'), may hold values from -4 to 4
- head_bias: float32 [3, 640], P(None, 'tp'), may hold values from -1 to 1
- hidden_bias: float32 [2560], P('tp'), may hold values from -1 to 1
- norm_vectors: float32 [6, 640], replicated, may hold values from -1 to 2
- attn_first: float32 [4, 640, 640], P(None, 'dp', 'tp')
- ffn_first: float32 [2, 640, 2560], P(None, 'dp', 'tp')
- head_first: float32 [3, 640], P(None, 'tp')
- hidden_first: float32 [2560], P('tp')
- vector_first: float32 [6, 640], replicated
- attn_second: float32 [4, 640, 640], P(None, 'dp', 'tp')
- ffn_second: float32 [2, 640, 2560], P(None, 'dp', 'tp')
- head_second: float32 [3, 640], P(None, 'tp')
- hidden_second: float32 [2560], P('tp')
- vector_second: float32 [6, 640], replicated
Outputs:
- layer_output: bfloat16 [32768, 640], P('dp')
- input_grad: bfloat16 [32768, 640], P('dp')
- new_attn_weights: float32 [4, 640, 640], P(None, 'dp', 'tp')
- new_ffn_weights: float32 [2, 640, 2560], P(None, 'dp', 'tp')
- new_head_bias: float32 [3, 640], P(None, 'tp')
- new_hidden_bias: float32 [2560], P('tp')
- new_norm_vectors: float32 [6, 640], replicated
- attn_first_new: float32 [4, 640, 640], P(None, 'dp', 'tp')
- ffn_first_new: float32 [2, 640, 2560], P(None, 'dp', 'tp')
- head_first_new: float32 [3, 640], P(None, 'tp')
- hidden_first_new: float32 [2560], P('tp')
- vector_first_new: float32 [6, 640], replicated
- attn_second_new: float32 [3, 640, 640], P(None, 'dp', 'tp')
- out_second_new: float32 [640, 640], P('dp', 'tp')
- ffn_second_new: float32 [2, 640, 2560], P(None, 'dp', 'tp')
- head_second_new: float32 [3, 640], P(None, 'tp')
- hidden_second_new: float32 [2560], P('tp')
- vector_second_new: float32 [4, 640], replicated
- norm_second_new: float32 [2, 640], replicated
- trust_norms: float32 [2, 16], replicated
Inputs may be any that keep to these rules, and one draw needn't show every extreme that they name: `segment_ids`: within each row of 1024 slots the ids never fall; each of the 6 ids forms one run of 1 to 400 slots, and one run has exactly 400 slots.
All inputs are finite; a program needn't handle non-finite values.
Results may differ from a plain program's by a relative error of at most 0.019.
Values may be sent and summed in bfloat16 or wider, within the bound.
No kernel may reach another device: no remote copies, remote signals or barrier semaphores. Data moves between devices by JAX's collectives and lax.ppermute only.
A program may use at most 192 MiB of HBM per device.

v0:
```python
from functools import partial

import jax
import jax.numpy as jnp
from jax import lax
from jax.sharding import PartitionSpec as P

HD = 32
STEP = 10


EPS_NORM = 1e-05
EPS_ADAM = 1e-06
BETA_ONE = 0.9
BETA_TWO = 0.999
DECAY = 0.01
RATE = 0.5
MASKED = -1e30


def layer_norm(values, scale_gain, offset):
    average = jnp.mean(values, axis=-1, keepdims=True)
    centered = values - average
    variance = jnp.mean(centered * centered, axis=-1, keepdims=True)
    return centered * lax.rsqrt(variance + EPS_NORM) * scale_gain + offset


def rope_tables(segments):
    slots_index = jnp.arange(segments.shape[0], dtype=jnp.int32)
    before = jnp.sum((segments[None, :] < segments[:, None]).astype(jnp.int32), axis=1)
    position = (slots_index - before).astype(jnp.float32)
    frequency = 10000.0 ** (-jnp.arange(0, HD, 2).astype(jnp.float32) / HD)
    angles = position[:, None] * frequency[None, :]
    angles = jnp.concatenate([angles, angles], axis=-1)
    return (jnp.cos(angles), jnp.sin(angles))


def rotate(values, cosine_table, sine_table):
    middle = values.shape[-1] // 2
    turned = jnp.concatenate([-values[..., middle:], values[..., :middle]], axis=-1)
    return values * cosine_table + turned * sine_table


def block_scores(queries, keys_row, same_protein):
    scores = jnp.einsum(
        "qhd,khd->hqk", queries, keys_row, preferred_element_type=jnp.float32
    ) * HD ** (-0.5)
    return jnp.where(same_protein[None], scores, MASKED)


def attend_block(queries, keys_row, values_row, same_protein):
    scores = block_scores(queries, keys_row, same_protein)
    highest = jnp.max(scores, axis=-1, keepdims=True)
    weights_exp = jnp.exp(scores - highest)
    row_total = jnp.sum(weights_exp, axis=-1, keepdims=True)
    attention = (weights_exp / row_total).astype(jnp.bfloat16)
    heads_out = jnp.einsum(
        "hqk,khd->qhd", attention, values_row, preferred_element_type=jnp.float32
    )
    return (heads_out, (highest + jnp.log(row_total))[..., 0])


def attend_block_back(queries, keys_row, values_row, same_protein, log_total, grad_heads):
    scores = block_scores(queries, keys_row, same_protein)
    attention = jnp.exp(scores - log_total[..., None])
    grad_values = jnp.einsum(
        "hqk,qhd->khd",
        attention.astype(jnp.bfloat16),
        grad_heads,
        preferred_element_type=jnp.float32,
    )
    grad_attention = jnp.einsum(
        "qhd,khd->hqk", grad_heads, values_row, preferred_element_type=jnp.float32
    )
    center = jnp.sum(attention * grad_attention, axis=-1, keepdims=True)
    grad_scores = (attention * (grad_attention - center)).astype(jnp.bfloat16)
    grad_queries = jnp.einsum(
        "hqk,khd->qhd", grad_scores, keys_row, preferred_element_type=jnp.float32
    ) * HD ** (-0.5)
    grad_keys = jnp.einsum(
        "hqk,qhd->khd", grad_scores, queries, preferred_element_type=jnp.float32
    ) * HD ** (-0.5)
    return (grad_queries, grad_keys, grad_values)


def attend_row(queries, keys_row, values_row, segments, block_rows):
    blocks = segments.shape[0] // block_rows
    query_blocks = queries.reshape((blocks, block_rows) + queries.shape[1:])
    segment_blocks = segments.reshape(blocks, block_rows)

    def one_block(packed):
        same_protein = packed[1][:, None] == segments[None, :]
        return attend_block(packed[0], keys_row, values_row, same_protein)

    heads_out, log_total = lax.map(one_block, (query_blocks, segment_blocks))
    return (heads_out.reshape(queries.shape), log_total)


def attend_row_back(queries, keys_row, values_row, segments, log_total, grad_heads, block_rows):
    blocks = segments.shape[0] // block_rows
    query_blocks = queries.reshape((blocks, block_rows) + queries.shape[1:])
    grad_blocks = grad_heads.reshape((blocks, block_rows) + grad_heads.shape[1:])
    segment_blocks = segments.reshape(blocks, block_rows)

    def one_block(totals, packed):
        same_protein = packed[1][:, None] == segments[None, :]
        grad_queries, grad_keys, grad_values = attend_block_back(
            packed[0], keys_row, values_row, same_protein, packed[2], packed[3]
        )
        return ((totals[0] + grad_keys, totals[1] + grad_values), grad_queries)

    zeros_rows = jnp.zeros(keys_row.shape, jnp.float32)
    sums_kv, grad_queries = lax.scan(
        one_block, (zeros_rows, zeros_rows), (query_blocks, segment_blocks, log_total, grad_blocks)
    )
    return (grad_queries.reshape(queries.shape), sums_kv[0], sums_kv[1])


def lamb_moments(weight, gradient, moment_one, moment_two):
    first_new = BETA_ONE * moment_one + (1.0 - BETA_ONE) * gradient
    second_new = BETA_TWO * moment_two + (1.0 - BETA_TWO) * gradient * gradient
    corrected = first_new / (1.0 - BETA_ONE**STEP)
    variance = second_new / (1.0 - BETA_TWO**STEP)
    update = corrected / (jnp.sqrt(variance) + EPS_ADAM) + DECAY * weight
    return (first_new, second_new, update)


def sum_squares(array):
    return jnp.sum(array * array, axis=tuple(range(1, array.ndim)))


def on_device(
    inputs,
    out_grad,
    segment_ids,
    attn_weights,
    ffn_weights,
    head_bias,
    hidden_bias,
    norm_vectors,
    attn_first,
    ffn_first,
    head_first,
    hidden_first,
    vector_first,
    attn_second,
    ffn_second,
    head_second,
    hidden_second,
    vector_second,
):
    data_count = lax.axis_size("dp")
    tensor_count = lax.axis_size("tp")
    row_count, slot_count = segment_ids.shape
    token_count = row_count * slot_count
    head_width = attn_weights.shape[2]
    local_heads = head_width // HD
    block_rows = min(512, slot_count)
    shard_rows = attn_weights.shape[1]
    masters = [attn_weights, ffn_weights, head_bias, hidden_bias.reshape(1, -1), norm_vectors]
    replicas = [1.0, 1.0, 1.0 / data_count, 1.0 / data_count, 1.0 / (data_count * tensor_count)]
    weight_terms = jnp.concatenate(
        [sum_squares(masters[member]) * replicas[member] for member in range(5)]
    )
    weight_sums = lax.psum(weight_terms, ("dp", "tp"))
    gathered_attn, gathered_ffn = (
        lax.all_gather(attn_weights.astype(jnp.bfloat16), "dp", axis=1, tiled=True),
        lax.all_gather(ffn_weights.astype(jnp.bfloat16), "dp", axis=1, tiled=True),
    )
    tables = jax.vmap(rope_tables)(segment_ids)
    cosine_table = tables[0][:, :, None, :]
    sine_table = tables[1][:, :, None, :]
    features = inputs.astype(jnp.float32)
    normed, norm_back = jax.vjp(layer_norm, features, norm_vectors[0], norm_vectors[1])
    normed_low = normed.astype(jnp.bfloat16)
    projected = jnp.einsum(
        "td,cdw->ctw", normed_low, gathered_attn[:3], preferred_element_type=jnp.float32
    )
    projected = projected + head_bias[:, None, :]
    shaped = projected.reshape(3, row_count, slot_count, local_heads, HD)
    turned, rotate_back = jax.vjp(lambda pair: rotate(pair, cosine_table, sine_table), shaped[:2])
    turned_low = turned.astype(jnp.bfloat16)
    values_low = shaped[2].astype(jnp.bfloat16)
    heads_out, log_total = lax.map(
        lambda packed: attend_row(packed[0], packed[1], packed[2], packed[3], block_rows),
        (turned_low[0], turned_low[1], values_low, segment_ids),
    )
    heads_low = heads_out.reshape(token_count, head_width).astype(jnp.bfloat16)
    out_projection = gathered_attn[3]
    attended = lax.psum(
        jnp.einsum(
            "tw,dw->td", heads_low, out_projection, preferred_element_type=jnp.float32
        ).astype(jnp.bfloat16),
        "tp",
    ).astype(jnp.float32)
    residual = features + attended + norm_vectors[2]
    normed_two, norm_two_back = jax.vjp(layer_norm, residual, norm_vectors[3], norm_vectors[4])
    normed_two_low = normed_two.astype(jnp.bfloat16)
    preact = (
        jnp.dot(normed_two_low, gathered_ffn[0], preferred_element_type=jnp.float32) + hidden_bias
    )
    activated, gelu_back = jax.vjp(partial(jax.nn.gelu, approximate=False), preact)
    activated_low = activated.astype(jnp.bfloat16)
    mixed_sum = lax.psum(
        jnp.einsum(
            "tf,df->td", activated_low, gathered_ffn[1], preferred_element_type=jnp.float32
        ).astype(jnp.bfloat16),
        "tp",
    ).astype(jnp.float32)
    layer_output = (residual + mixed_sum + norm_vectors[5]).astype(jnp.bfloat16)
    grad_output = out_grad.astype(jnp.float32)
    grad_down = jnp.einsum("td,tf->df", out_grad, activated_low, preferred_element_type=jnp.float32)
    grad_act = jnp.einsum(
        "td,df->tf", out_grad, gathered_ffn[1], preferred_element_type=jnp.float32
    )
    grad_pre = gelu_back(grad_act)[0].astype(jnp.bfloat16)
    grad_up = jnp.einsum("td,tf->df", normed_two_low, grad_pre, preferred_element_type=jnp.float32)
    grad_hidden_bias = jnp.sum(grad_pre.astype(jnp.float32), axis=0)
    grad_normed_two = lax.psum(
        jnp.einsum(
            "tf,df->td", grad_pre, gathered_ffn[0], preferred_element_type=jnp.float32
        ).astype(jnp.bfloat16),
        "tp",
    ).astype(jnp.float32)
    grad_residual_ln, grad_gain_two, grad_shift_two = norm_two_back(grad_normed_two)
    grad_residual = grad_output + grad_residual_ln
    grad_residual_low = grad_residual.astype(jnp.bfloat16)
    grad_out_projection = jnp.einsum(
        "td,tw->dw", grad_residual_low, heads_low, preferred_element_type=jnp.float32
    )
    grad_heads = jnp.einsum(
        "td,dw->tw", grad_residual_low, out_projection, preferred_element_type=jnp.float32
    )
    grad_heads = grad_heads.astype(jnp.bfloat16).reshape(row_count, slot_count, local_heads, HD)
    grad_turned_q, grad_turned_k, grad_values = lax.map(
        lambda packed: attend_row_back(
            packed[0], packed[1], packed[2], packed[3], packed[4], packed[5], block_rows
        ),
        (turned_low[0], turned_low[1], values_low, segment_ids, log_total, grad_heads),
    )
    grad_shaped_qk = rotate_back(jnp.stack([grad_turned_q, grad_turned_k]))[0]
    grad_projected = jnp.concatenate([grad_shaped_qk, grad_values[None]], axis=0)
    grad_projected = grad_projected.reshape(3, token_count, head_width).astype(jnp.bfloat16)
    grad_head_bias = jnp.sum(grad_projected.astype(jnp.float32), axis=1)
    grad_qkv = jnp.einsum(
        "td,ctw->cdw", normed_low, grad_projected, preferred_element_type=jnp.float32
    )
    grad_normed = lax.psum(
        jnp.einsum(
            "ctw,cdw->td", grad_projected, gathered_attn[:3], preferred_element_type=jnp.float32
        ).astype(jnp.bfloat16),
        "tp",
    ).astype(jnp.float32)
    grad_features_ln, grad_gain, grad_shift = norm_back(grad_normed)
    input_grad = (grad_residual + grad_features_ln).astype(jnp.bfloat16)
    grad_vectors = jnp.stack(
        [
            grad_gain,
            grad_shift,
            jnp.sum(grad_residual, axis=0),
            grad_gain_two,
            grad_shift_two,
            jnp.sum(grad_output, axis=0),
        ]
    )
    grad_attn = jnp.concatenate([grad_qkv, grad_out_projection[None]], axis=0)
    grad_ffn = jnp.stack([grad_up, grad_down])
    full_attn, full_ffn, sum_head, sum_hidden, sum_vectors = lax.psum(
        (grad_attn, grad_ffn, grad_head_bias, grad_hidden_bias, grad_vectors), "dp"
    )
    offset_rows = lax.axis_index("dp") * shard_rows
    own_attn = lax.dynamic_slice_in_dim(full_attn, offset_rows, shard_rows, 1)
    own_ffn = lax.dynamic_slice_in_dim(full_ffn, offset_rows, shard_rows, 1)
    grads_list = [own_attn, own_ffn, sum_head, sum_hidden.reshape(1, -1), sum_vectors]
    firsts = [attn_first, ffn_first, head_first, hidden_first.reshape(1, -1), vector_first]
    seconds = [attn_second, ffn_second, head_second, hidden_second.reshape(1, -1), vector_second]
    results = [
        lamb_moments(masters[member], grads_list[member], firsts[member], seconds[member])
        for member in range(5)
    ]
    update_terms = jnp.concatenate(
        [sum_squares(results[member][2]) * replicas[member] for member in range(5)]
    )
    update_sums = lax.psum(update_terms, ("dp", "tp"))
    weight_norms = jnp.sqrt(weight_sums)
    update_norms = jnp.sqrt(update_sums)
    trust_ratio = weight_norms / update_norms
    counts = [4, 2, 3, 1, 6]
    new_weights = []
    begin_at = 0
    for member in range(5):
        piece_ratio = trust_ratio[begin_at : begin_at + counts[member]]
        shaped_ratio = piece_ratio.reshape((-1,) + (1,) * (masters[member].ndim - 1))
        new_weights.append(masters[member] - RATE * shaped_ratio * results[member][2])
        begin_at += counts[member]
    return (
        layer_output,
        input_grad,
        new_weights[0],
        new_weights[1],
        new_weights[2],
        new_weights[3].reshape(-1),
        new_weights[4],
        results[0][0],
        results[1][0],
        results[2][0],
        results[3][0].reshape(-1),
        results[4][0],
        results[0][1][:3],
        results[0][1][3],
        results[1][1],
        results[2][1],
        results[3][1].reshape(-1),
        results[4][1][2:],
        results[4][1][:2],
        jnp.stack([weight_norms, update_norms]),
    )


def solution(mesh):
    in_specs = (
        P("dp", None),
        P("dp", None),
        P("dp", None),
        P(None, "dp", "tp"),
        P(None, "dp", "tp"),
        P(None, "tp"),
        P("tp"),
        P(),
        P(None, "dp", "tp"),
        P(None, "dp", "tp"),
        P(None, "tp"),
        P("tp"),
        P(),
        P(None, "dp", "tp"),
        P(None, "dp", "tp"),
        P(None, "tp"),
        P("tp"),
        P(),
    )
    out_specs = (
        P("dp", None),
        P("dp", None),
        P(None, "dp", "tp"),
        P(None, "dp", "tp"),
        P(None, "tp"),
        P("tp"),
        P(),
        P(None, "dp", "tp"),
        P(None, "dp", "tp"),
        P(None, "tp"),
        P("tp"),
        P(),
        P(None, "dp", "tp"),
        P("dp", "tp"),
        P(None, "dp", "tp"),
        P(None, "tp"),
        P("tp"),
        P(),
        P(),
        P(),
    )
    return jax.shard_map(
        on_device, mesh=mesh, in_specs=in_specs, out_specs=out_specs, check_vma=False
    )
```

profile of v0, /device:TPU:0, one launch (start us, length us, event | category | flops | bytes accessed | tf_op | source)
XLA Modules:
  0.0 1303.6 jit_solution(11081138493760027001)
XLA Ops:
  17.8 36.7 %all-gather.3.cloned.1.call-done = bf16[4,640,320]{2,0,1:T(4,128)(2,1)} async-done(((bf16[4,40,320]{2,0,1:T(4,128)(2,1)}), bf16[4,640,320]{2,0,1:T(4,128)(2,1)}) %all-gather.3.cloned.1.call-update) | async-done | bytes 1638416 | tf_op jit(solution)/shard_map/all_gather | solution.py:167
  90.6 138.8 %while.54 = (s32[]{:T(128)}, bf16[2,1024,10,32]{3,2,1,0:T(8,128)(2,1)}, f32[2,2,10,512]{3,2,1,0:T(8,128)}, bf16[2,1024,10,32]{1,3,2,0:T(8,128)(2,1)S(1)}, s32[2,...) while((s32[]{:T(128)}, ...), condition=%wide.region_8.0_spmd, body=%wide.region_3.8_spmd.sunk | while | flops 734522368 | bytes 181594624 | solution.py:184
  95.4 54.8 %while.57 = (s32[]{:T(128)}, bf16[2,512,10,32]{1,3,2,0:T(8,128)(2,1)S(1)}, f32[2,10,512]{2,1,0:T(8,128)S(1)}, s32[2,512]{1,0:T(2,128)S(1)}, s32[1024]{0:T(1024)S...) while((s32[]{:T(128)}, ...), condition=%wide.region_7.7_spmd, body=%wide.region_4.6_spmd.sunk | while | flops 734522368 | bytes 154048688 | solution.py:95
  164.8 54.8 %while.57 = (s32[]{:T(128)}, bf16[2,512,10,32]{1,3,2,0:T(8,128)(2,1)S(1)}, f32[2,10,512]{2,1,0:T(8,128)S(1)}, s32[2,512]{1,0:T(2,128)S(1)}, s32[1024]{0:T(1024)S...) while((s32[]{:T(128)}, ...), condition=%wide.region_7.7_spmd, body=%wide.region_4.6_spmd.sunk | while | flops 734522368 | bytes 154048688 | solution.py:95
  246.1 72.6 %all-reduce.11.cloned.1.call-done = bf16[2048,640]{1,0:T(8,128)(2,1)} async-done(((bf16[2048,640]{1,0:T(8,128)(2,1)}), bf16[2048,640]{1,0:T(8,128)(2,1)}) %all-reduce.11.cloned.1.call-update) | async-done | bytes 2621456 | tf_op jit(solution)/shard_map/psum | solution.py:190
  323.0 44.8 %all-gather.5.cloned.1.call-done = bf16[2,640,1280]{2,1,0:T(8,128)(2,1)} async-done(((bf16[2,40,1280]{2,1,0:T(8,128)(2,1)}), bf16[2,640,1280]{2,1,0:T(8,128)(2,1)}) %all-gather.5.cloned.1.call-update) | async-done | bytes 3276816 | tf_op jit(solution)/shard_map/all_gather | solution.py:168
  367.8 31.1 %multiply_convert_fusion.1 = (bf16[2048,1280]{1,0:T(8,128)(2,1)}, f32[2048,1280]{1,0:T(8,128)}, f32[2048,1280]{1,0:T(8,128)}) fusion(f32[1280]{0:T(1024)S(1)} %copy-done.50, bf16[2,640,1280]{2,1,0:T(8,128)(2,1)} %all-gather.5.cloned.1.call-done, f32[640]{0:T(1024)S(1)} %copy-done.58, f32[640]{0:T(1024)S(1)} %copy-done.47, f32[2048]{0:T(1024)S(1)} %fusion.84, ...), kind=kOutput, calls=%fused_computation.69 | convolution fusion | flops 3540254720 | bytes 33124864 | tf_op jit(solution)/shard_map/dot_general | solution.py:200
  398.9 12.4 convert_reduce_fusion
  434.7 58.3 %all-reduce.13.cloned.1.call-done = bf16[2048,640]{1,0:T(8,128)(2,1)} async-done(((bf16[2048,640]{1,0:T(8,128)(2,1)}), bf16[2048,640]{1,0:T(8,128)(2,1)}) %all-reduce.13.cloned.1.call-update) | async-done | bytes 2621456 | tf_op jit(solution)/shard_map/psum | solution.py:219
  512.9 277.2 %while.56 = (s32[]{:T(128)}, f32[2,1024,10,32]{1,3,2,0:T(8,128)}, f32[2,1024,10,32]{1,3,2,0:T(8,128)}, bf16[2,1024,10,32]{1,3,2,0:T(8,128)(2,1)}, bf16[2,1024,10...) while((s32[]{:T(128)}, f32[2,1024,10,32]{1,3,2,0:T(8,128)}, ...), condition=%wide.region_20.21_spmd, body=%wide.region_16.20_spmd.sunk | while | flops 1758686208 | bytes 284158464 | solution.py:235
  524.7 111.2 %while.58 = (s32[]{:T(128)}, f32[1024,10,32]{0,2,1:T(8,128)S(1)}, f32[1024,10,32]{0,2,1:T(8,128)}, f32[2,512,10,32]{1,3,2,0:T(8,128)}, bf16[2,512,10,32]{1,3,2,0...) while((s32[]{:T(128)}, f32[1024,10,32]{0,2,1:T(8,128)S(1)}, ...), condition=%wide.region_19.19_spmd.clone, body=%wide.region_17.18_spmd.clone.sunk | while | flops 1758686208 | bytes 255219920 | solution.py:113
  544.4 15.2 %multiply_reduce_fusion.13 = (f32[10,512]{1,0:T(8,128)S(1)}, f32[10,512,1024]{2,1,0:T(8,128)}) fusion(f32[10,512,1024]{2,1,0:T(8,128)} %copy-done, f32[10,512]{1,0:T(8,128)S(1)} %dynamic-slice_bitcast_fusion.15, pred[512,1024]{1,0:T(8,128)(4,1)S(1)} %broadcast_compare_fusion.4, bf16[1024,10,32]{0,2,1:T(8,128)(2,1)} %get-tuple-element.1035, ...), kind=kOutput, calls=%fused_computation.18.clone.1 | convolution fusion | flops 361753600 | bytes 43491332 | tf_op jit(solution)/shard_map/while/body/eval_jaxpr/while/body/eval_jaxpr/qhd,khd->hqk/dot_general | solution.py:72
  559.5 14.6 %multiply_convert_fusion.3 = bf16[10,512,1024]{2,1,0:T(8,128)(2,1)S(1)} fusion(f32[10,512,1024]{2,1,0:T(8,128)} %get-tuple-element.987, f32[10,512,1024]{2,1,0:T(8,128)} %copy-done, f32[10,512]{1,0:T(8,128)S(1)} %get-tuple-element.988, f32[10,512]{1,0:T(8,128)S(1)} %dynamic-slice_bitcast_fusion.15, pred[512,1024]{1,0:T(8,128)(4,1)S(1)} %broadcast_compare_fusion.4), kind=kLoop, calls=%fused_computation.17.clone.1 | loop fusion | flops 31457280 | bytes 52994048 | tf_op jit(solution)/shard_map/while/body/eval_jaxpr/while/body/eval_jaxpr/convert_element_type | solution.py:76
  600.1 15.2 %multiply_reduce_fusion.13 = (f32[10,512]{1,0:T(8,128)S(1)}, f32[10,512,1024]{2,1,0:T(8,128)}) fusion(f32[10,512,1024]{2,1,0:T(8,128)} %copy-done, f32[10,512]{1,0:T(8,128)S(1)} %dynamic-slice_bitcast_fusion.15, pred[512,1024]{1,0:T(8,128)(4,1)S(1)} %broadcast_compare_fusion.4, bf16[1024,10,32]{0,2,1:T(8,128)(2,1)} %get-tuple-element.1035, ...), kind=kOutput, calls=%fused_computation.18.clone.1 | convolution fusion | flops 361753600 | bytes 43491332 | tf_op jit(solution)/shard_map/while/body/eval_jaxpr/while/body/eval_jaxpr/qhd,khd->hqk/dot_general | solution.py:72
  615.3 14.6 %multiply_convert_fusion.3 = bf16[10,512,1024]{2,1,0:T(8,128)(2,1)S(1)} fusion(f32[10,512,1024]{2,1,0:T(8,128)} %get-tuple-element.987, f32[10,512,1024]{2,1,0:T(8,128)} %copy-done, f32[10,512]{1,0:T(8,128)S(1)} %get-tuple-element.988, f32[10,512]{1,0:T(8,128)S(1)} %dynamic-slice_bitcast_fusion.15, pred[512,1024]{1,0:T(8,128)(4,1)S(1)} %broadcast_compare_fusion.4), kind=kLoop, calls=%fused_computation.17.clone.1 | loop fusion | flops 31457280 | bytes 52994048 | tf_op jit(solution)/shard_map/while/body/eval_jaxpr/while/body/eval_jaxpr/convert_element_type | solution.py:76
  663.0 111.2 %while.58 = (s32[]{:T(128)}, f32[1024,10,32]{0,2,1:T(8,128)S(1)}, f32[1024,10,32]{0,2,1:T(8,128)}, f32[2,512,10,32]{1,3,2,0:T(8,128)}, bf16[2,512,10,32]{1,3,2,0...) while((s32[]{:T(128)}, f32[1024,10,32]{0,2,1:T(8,128)S(1)}, ...), condition=%wide.region_19.19_spmd.clone, body=%wide.region_17.18_spmd.clone.sunk | while | flops 1758686208 | bytes 255219920 | solution.py:113
  682.7 15.2 %multiply_reduce_fusion.13 = (f32[10,512]{1,0:T(8,128)S(1)}, f32[10,512,1024]{2,1,0:T(8,128)}) fusion(f32[10,512,1024]{2,1,0:T(8,128)} %copy-done, f32[10,512]{1,0:T(8,128)S(1)} %dynamic-slice_bitcast_fusion.15, pred[512,1024]{1,0:T(8,128)(4,1)S(1)} %broadcast_compare_fusion.4, bf16[1024,10,32]{0,2,1:T(8,128)(2,1)} %get-tuple-element.1035, ...), kind=kOutput, calls=%fused_computation.18.clone.1 | convolution fusion | flops 361753600 | bytes 43491332 | tf_op jit(solution)/shard_map/while/body/eval_jaxpr/while/body/eval_jaxpr/qhd,khd->hqk/dot_general | solution.py:72
  697.8 14.6 %multiply_convert_fusion.3 = bf16[10,512,1024]{2,1,0:T(8,128)(2,1)S(1)} fusion(f32[10,512,1024]{2,1,0:T(8,128)} %get-tuple-element.987, f32[10,512,1024]{2,1,0:T(8,128)} %copy-done, f32[10,512]{1,0:T(8,128)S(1)} %get-tuple-element.988, f32[10,512]{1,0:T(8,128)S(1)} %dynamic-slice_bitcast_fusion.15, pred[512,1024]{1,0:T(8,128)(4,1)S(1)} %broadcast_compare_fusion.4), kind=kLoop, calls=%fused_computation.17.clone.1 | loop fusion | flops 31457280 | bytes 52994048 | tf_op jit(solution)/shard_map/while/body/eval_jaxpr/while/body/eval_jaxpr/convert_element_type | solution.py:76
  738.4 15.2 %multiply_reduce_fusion.13 = (f32[10,512]{1,0:T(8,128)S(1)}, f32[10,512,1024]{2,1,0:T(8,128)}) fusion(f32[10,512,1024]{2,1,0:T(8,128)} %copy-done, f32[10,512]{1,0:T(8,128)S(1)} %dynamic-slice_bitcast_fusion.15, pred[512,1024]{1,0:T(8,128)(4,1)S(1)} %broadcast_compare_fusion.4, bf16[1024,10,32]{0,2,1:T(8,128)(2,1)} %get-tuple-element.1035, ...), kind=kOutput, calls=%fused_computation.18.clone.1 | convolution fusion | flops 361753600 | bytes 43491332 | tf_op jit(solution)/shard_map/while/body/eval_jaxpr/while/body/eval_jaxpr/qhd,khd->hqk/dot_general | solution.py:72
  753.6 14.6 %multiply_convert_fusion.3 = bf16[10,512,1024]{2,1,0:T(8,128)(2,1)S(1)} fusion(f32[10,512,1024]{2,1,0:T(8,128)} %get-tuple-element.987, f32[10,512,1024]{2,1,0:T(8,128)} %copy-done, f32[10,512]{1,0:T(8,128)S(1)} %get-tuple-element.988, f32[10,512]{1,0:T(8,128)S(1)} %dynamic-slice_bitcast_fusion.15, pred[512,1024]{1,0:T(8,128)(4,1)S(1)} %broadcast_compare_fusion.4), kind=kLoop, calls=%fused_computation.17.clone.1 | loop fusion | flops 31457280 | bytes 52994048 | tf_op jit(solution)/shard_map/while/body/eval_jaxpr/while/body/eval_jaxpr/convert_element_type | solution.py:76
  839.9 181.4 %all-reduce.15.cloned.1.call-done = (f32[4,640,320]{2,1,0:T(8,128)}, f32[2,640,1280]{2,1,0:T(8,128)}) async-done(((f32[4,640,320]{2,1,0:T(8,128)}, f32[2,640,1280]{2,1,0:T(8,128)}), (f32[4,640,320]{2,1,0:T(8,128)}, f32[2,640,1280]{2,1,0:T(8,128)})) %all-reduce.15.cloned.1.call-update) | async-done | bytes 9830416 | tf_op jit(solution)/shard_map/psum | solution.py:268
  1027.6 127.7 %all-reduce.17.cloned.1.call-done = (bf16[2048,640]{1,0:T(8,128)(2,1)}, bf16[2048,640]{1,0:T(8,128)(2,1)}) async-done(((bf16[2048,640]{1,0:T(8,128)(2,1)}, bf16[2048,640]{1,0:T(8,128)(2,1)}), (bf16[2048,640]{1,0:T(8,128)(2,1)}, bf16[2048,640]{1,0:T(8,128)(2,1)})) %all-reduce.17.cloned.1.call-update) | async-done | bytes 5242896 | tf_op jit(solution)/shard_map/psum | solution.py:204
  1164.4 62.5 %all-reduce.3 = (f32[3,320]{1,0:T(4,128)}, f32[1280]{0:T(1024)}, f32[6,640]{1,0:T(8,128)}) all-reduce(f32[3,320]{1,0:T(4,128)} %convert_reduce_fusion.2, f32[1280]{0:T(1024)} %get-tuple-element.699, f32[6,640]{1,0:T(8,128)S(1)} %stack.48), channel_id=1, replica_groups=mesh['dp'=16,'tp'=2] {'dp'}, use_global_device_ids=true, to_apply=%region_35.36 | all-reduce | flops 6080 | bytes 48640 | tf_op jit(solution)/shard_map/psum | solution.py:268
  1237.4 37.1 %all-reduce.2 = (f32[16]{0:T(128)}, f32[16]{0:T(128)}) all-reduce(f32[16]{0:T(128)} %concatenate.39, f32[16]{0:T(128)} %concatenate.37), channel_id=1, replica_groups=mesh['dp'=16,'tp'=2] {'dp','tp'}, use_global_device_ids=true, to_apply=%region_48.49 | all-reduce | flops 32 | bytes 256 | tf_op jit(solution)/shard_map/psum | solution.py:284
  (389 shorter events, 501.8 us)
Async XLA Ops:
  7.2 51.8 %copy-start.51 = (f32[3,320]{1,0:T(4,128)S(1)}, f32[3,320]{1,0:T(4,128)}, u32[]{:S(2)}) copy-start(f32[3,320]{1,0:T(4,128)} %param.31) | copy-start | bytes 11524
  7.2 47.3 %all-gather.3.cloned.1.call-start = ((), (), s32[]{:S(2)}) async-start(), calls=%async_computation | async-start | bytes 2088960 | tf_op jit(solution)/shard_map/all_gather | solution.py:167
  9.1 309.6 %all-reduce.11.cloned.1.call-start = ((), (), s32[]{:S(2)}) async-start(), calls=%async_computation.1 | async-start | bytes 5242880 | tf_op jit(solution)/shard_map/psum | solution.py:190
  10.8 53.0 %copy-start.48 = (f32[640]{0:T(1024)}, f32[640]{0:T(1024)S(1)}, u32[]{:S(2)}) copy-start(f32[640]{0:T(1024)S(1)} %get-tuple-element.571) | copy-start | bytes 7684
  10.8 53.0 %copy-start.56 = (f32[640]{0:T(1024)}, f32[640]{0:T(1024)S(1)}, u32[]{:S(2)}) copy-start(f32[640]{0:T(1024)S(1)} %get-tuple-element.570) | copy-start | bytes 7684
  13.8 72.1 %copy-start.29 = (f32[2,1024,32]{1,2,0:T(8,128)}, f32[2,1024,32]{1,2,0:T(8,128)S(1)}, u32[]{:S(2)}) copy-start(f32[2,1024,32]{1,2,0:T(8,128)S(1)} %get-tuple-element.692) | copy-start | bytes 786436
  13.8 72.1 %copy-start.31 = (f32[2,1024,32]{1,2,0:T(8,128)}, f32[2,1024,32]{1,2,0:T(8,128)S(1)}, u32[]{:S(2)}) copy-start(f32[2,1024,32]{1,2,0:T(8,128)S(1)} %get-tuple-element.693) | copy-start | bytes 786436
  16.2 47.7 %copy-start.38 = (f32[2048]{0:T(1024)}, f32[2048]{0:T(1024)S(1)}, u32[]{:S(2)}) copy-start(f32[2048]{0:T(1024)S(1)} %broadcast_multiply_fusion.2) | copy-start | bytes 24580
  17.8 46.0 %copy-start.43 = (f32[2048]{0:T(1024)}, f32[2048]{0:T(1024)S(1)}, u32[]{:S(2)}) copy-start(f32[2048]{0:T(1024)S(1)} %fusion.83) | copy-start | bytes 24580
  95.4 54.8 %copy-start.36 = (f32[2,2,10,512]{3,2,1,0:T(8,128)S(1)}, f32[2,2,10,512]{3,2,1,0:T(8,128)}, u32[]{:S(2)}) copy-start(f32[2,2,10,512]{3,2,1,0:T(8,128)} %get-tuple-element.1077) | copy-start | bytes 245764 | tf_op jit(solution)/shard_map/while
  164.8 54.8 %copy-start.36 = (f32[2,2,10,512]{3,2,1,0:T(8,128)S(1)}, f32[2,2,10,512]{3,2,1,0:T(8,128)}, u32[]{:S(2)}) copy-start(f32[2,2,10,512]{3,2,1,0:T(8,128)} %get-tuple-element.1077) | copy-start | bytes 245764 | tf_op jit(solution)/shard_map/while
  240.5 78.2 %copy-start.4 = (bf16[2048,640]{1,0:T(8,128)(2,1)S(1)}, bf16[2048,640]{1,0:T(8,128)(2,1)}, u32[]{:S(2)}) copy-start(bf16[2048,640]{1,0:T(8,128)(2,1)} %param.26) | copy-start | bytes 7864324
  240.5 78.2 %copy-start.40 = (f32[640]{0:T(1024)S(1)}, f32[640]{0:T(1024)}, u32[]{:S(2)}) copy-start(f32[640]{0:T(1024)} %get-tuple-element.569) | copy-start | bytes 7684
  245.3 122.5 %all-gather.5.cloned.1.call-start = ((), (), s32[]{:S(2)}) async-start(), calls=%async_computation.2 | async-start | bytes 3481600 | tf_op jit(solution)/shard_map/all_gather | solution.py:168
  246.1 246.9 %all-reduce.13.cloned.1.call-start = ((), (), s32[]{:S(2)}) async-start(), calls=%async_computation.3 | async-start | bytes 5242880 | tf_op jit(solution)/shard_map/psum | solution.py:219
  318.7 49.1 %copy-start.47 = (f32[640]{0:T(1024)S(1)}, f32[640]{0:T(1024)}, u32[]{:S(2)}) copy-start(f32[640]{0:T(1024)} %get-tuple-element.568) | copy-start | bytes 7684
  318.7 49.1 %copy-start.50 = (f32[1280]{0:T(1024)S(1)}, f32[1280]{0:T(1024)}, u32[]{:S(2)}) copy-start(f32[1280]{0:T(1024)} %param.32) | copy-start | bytes 15364
  318.7 49.1 %copy-start.58 = (f32[640]{0:T(1024)S(1)}, f32[640]{0:T(1024)}, u32[]{:S(2)}) copy-start(f32[640]{0:T(1024)} %get-tuple-element.567) | copy-start | bytes 7684
  419.6 601.7 %all-reduce.15.cloned.1.call-start = ((), (), s32[]{:S(2)}) async-start(), calls=%async_computation.4 | async-start | bytes 20971520 | tf_op jit(solution)/shard_map/psum | solution.py:268
  819.6 335.7 %all-reduce.17.cloned.1.call-start = ((), (), s32[]{:S(2)}) async-start(), calls=%async_computation.5 | async-start | bytes 10485760 | tf_op jit(solution)/shard_map/psum | solution.py:204
  833.6 187.7 %copy-start.33 = (f32[4,40,320]{2,1,0:T(8,128)S(1)}, f32[4,40,320]{2,1,0:T(8,128)}, u32[]{:S(2)}) copy-start(f32[4,40,320]{2,1,0:T(8,128)} %param.29) | copy-start | bytes 614404
  833.6 191.0 %copy-start.26 = (f32[2,40,1280]{2,1,0:T(8,128)S(1)}, f32[2,40,1280]{2,1,0:T(8,128)}, u32[]{:S(2)}) copy-start(f32[2,40,1280]{2,1,0:T(8,128)} %param.30) | copy-start | bytes 1228804
  839.9 319.4 %copy-start.46 = (f32[2048]{0:T(1024)S(1)}, f32[2048]{0:T(1024)}, u32[]{:S(2)}) copy-start(f32[2048]{0:T(1024)} %copy-done.45) | copy-start | bytes 24580
  1158.7 128.4 %copy-start.41 = (f32[640]{0:T(1024)S(1)}, f32[640]{0:T(1024)}, u32[]{:S(2)}) copy-start(f32[640]{0:T(1024)} %get-tuple-element.569) | copy-start | bytes 7684
  (63 other events, 401.0 us)
Sparse Core Ops, SparseCore 0:
  10.9 43.5 all-gather.2
  245.4 73.2 all-reduce.10
  321.7 46.0 all-gather.4
  419.8 73.1 all-reduce.12
  819.7 201.5 all-reduce.14
  1024.4 130.8 all-reduce.16
where the time goes:
time: 1320 us; the launch traced here: 1300 us
  waiting for transfers between devices  522 us (40%)
  matrix products  279 us (21%)
  local copies, waits for them, and re-layouts  218 us (17%)
  other arithmetic  167 us (13%)
  blocking collectives  99.6 us (8%)
  between operations  17 us (1%)
    psum x1, waiting for transfers between devices, on_device(): lax.psum((grad_attn, grad_ffn, grad_head_bias, grad_hidden_bias, grad_vec...  181 us
    psum x1, waiting for transfers between devices, on_device(): lax.psum(jnp.einsum('tf,df->td', activated_low, gathered_ffn[1], preferre...  128 us
    psum x1, waiting for transfers between devices, on_device(): lax.psum(jnp.einsum('tw,dw->td', heads_low, out_projection, preferred_ele...  72.6 us
    psum x1, blocking collectives, on_device(): lax.psum((grad_attn, grad_ffn, grad_head_bias, grad_hidden_bias, grad_vec...  62.5 us
    dot_general x4, matrix products, attend_block_back(): jnp.einsum('qhd,khd->hqk', grad_heads, values_row, preferred_element_type...  60.6 us
    while x56, local copies, waits for them, and re-layouts  59.7 us
    convert_element_type x4, other arithmetic, attend_block_back(): grad_scores = (attention * (grad_attention - center)).astype(jnp.bfloat16)  58.3 us
    psum x1, waiting for transfers between devices, on_device(): lax.psum(jnp.einsum('tf,df->td', grad_pre, gathered_ffn[0], preferred_ele...  58.3 us
  transfers between devices with their start and end apart: 6, of which 6 were waited for; matrix products, arithmetic and copies ran while one was open for 4% of the time, Pallas kernels for 0%

commit v1 on v0

v1 whole, which is shorter than its diff:
```python
import math

import jax
import jax.numpy as jnp
from jax import lax
from jax.experimental import pallas as pl
from jax.experimental.pallas import tpu as pltpu
from jax.sharding import PartitionSpec as P

STEP = 10
EPS_NORM = 1e-05
EPS_ADAM = 1e-06
BETA_ONE = 0.9
BETA_TWO = 0.999
DECAY = 0.01
RATE = 0.5
HD=32
BIG=1e30
QT=128
KC=256
QSCALE=math.log2(math.e)/math.sqrt(HD)
LN2=math.log(2.0)
VM=56*1024*1024
bf=jnp.bfloat16
f32=jnp.float32

def dg(a,b,ca,cb):
    return lax.dot_general(a,b,(((ca,),(cb,)),((),())),preferred_element_type=f32)

def rope_rows(y,cos,sin,heads,sign):
    out=[]
    for h in range(heads):
        top=y[HD*h:HD*h+HD//2]; bot=y[HD*h+HD//2:HD*h+HD]
        out.append(top*cos-sign*bot*sin); out.append(bot*cos+sign*top*sin)
    return jnp.concatenate(out,axis=0)

def fwd_body(rng_ref,n1_ref,w_ref,b_ref,cos_ref,sin_ref,fq_ref,fk_ref,
             qt_ref,kt_ref,kp_ref,vn_ref,ot_ref,lse_ref,vt_ref,qbd_ref):
    width=w_ref.shape[2]; heads=width//HD; groups=heads//2; T=n1_ref.shape[0]; pad=kt_ref.shape[1]-T
    cos=cos_ref[...]; sin=sin_ref[...]
    n1=n1_ref[...]
    for c in range(3):
        y=dg(w_ref[c],n1,0,1)+b_ref[:,c:c+1]
        if c<2: y=rope_rows(y,cos,sin,heads,1.0)
        if c==0: qt_ref[...]=(y*QSCALE).astype(bf)
        elif c==1:
            yb=y.astype(bf)
            kt_ref[:,:T]=yb
            kt_ref[:,T:]=jnp.zeros((width,pad),bf)
            fk=fk_ref[...].astype(f32)
            for g in range(groups):
                piece=jnp.concatenate([y[64*g:64*g+64],fk[:,:T]],axis=0)
                kp_ref[g,:T,:]=jnp.transpose(piece).astype(bf)
                kp_ref[g,T:,:]=jnp.transpose(jnp.concatenate([jnp.zeros((64,pad),f32),fk[:,T:]],axis=0)).astype(bf)
        else:
            yb=y.astype(bf)
            ones=jnp.ones((16,T+pad),bf)
            for h in range(heads):
                vt_ref[h,:HD,:T]=yb[HD*h:HD*h+HD]
                vt_ref[h,:HD,T:]=jnp.zeros((HD,pad),bf)
                vt_ref[h,HD:,:]=ones
            for g in range(groups):
                piece=jnp.concatenate([y[64*g:64*g+64],jnp.zeros((64,T),f32)],axis=0)
                vn_ref[g,:T,:]=jnp.transpose(piece).astype(bf)
                vn_ref[g,T:,:]=jnp.zeros((pad,128),bf)
    z32=jnp.zeros((HD,QT),bf)
    def qtile(i,_):
        q0=pl.multiple_of(i*QT,QT)
        lo=rng_ref[0,i]; n=rng_ref[1,i]
        fq=fq_ref[:,pl.ds(q0,QT)]
        for g in range(groups):
            q=qt_ref[64*g:64*g+64,pl.ds(q0,QT)]
            left=jnp.concatenate([q[:HD],z32,fq],axis=0)
            right=jnp.concatenate([z32,q[HD:],fq],axis=0)
            qbd_ref[g]=jnp.concatenate([left,right],axis=1)
        def chunk(j,carry):
            k0=pl.multiple_of(lo*128+j*KC,128)
            new=[]
            for g in range(groups):
                m,acc=carry[g]
                s=jnp.dot(kp_ref[g,pl.ds(k0,KC),:],qbd_ref[g],preferred_element_type=f32)
                mn=jnp.maximum(m,jnp.max(s,axis=0,keepdims=True))
                al=jnp.exp2(m-mn)
                p=jnp.exp2(s-mn).astype(bf)
                outs=[]
                for a in range(2):
                    pv=jnp.dot(vt_ref[2*g+a,:,pl.ds(k0,KC)],p[:,QT*a:QT*a+QT],preferred_element_type=f32)
                    outs.append(acc[a]*al[:,QT*a:QT*a+QT]+pv)
                new.append((mn,tuple(outs)))
            return tuple(new)
        init=tuple((jnp.full((1,2*QT),-3e38,f32),(jnp.zeros((48,QT),f32),jnp.zeros((48,QT),f32))) for g in range(groups))
        res=lax.fori_loop(0,n,chunk,init)
        for g in range(groups):
            m,acc=res[g]
            for a in range(2):
                h=2*g+a
                l=acc[a][HD:HD+1]
                ot_ref[HD*h:HD*h+HD,pl.ds(q0,QT)]=(acc[a][:HD]/l).astype(bf)
                lse_ref[h:h+1,pl.ds(q0,QT)]=m[:,QT*a:QT*a+QT]+jnp.log2(l)
        return 0
    lax.fori_loop(0,T//QT,qtile,0)

def attn_fwd(rng,n1,w,b,cos,sin,fq,fk):
    T=n1.shape[0]; width=w.shape[2]; heads=width//HD; groups=heads//2; TP=T+128
    V=pl.BlockSpec(memory_space=pltpu.VMEM); S=pl.BlockSpec(memory_space=pltpu.SMEM)
    return pl.pallas_call(fwd_body,
        out_shape=(jax.ShapeDtypeStruct((width,T),bf),jax.ShapeDtypeStruct((width,TP),bf),jax.ShapeDtypeStruct((groups,TP,128),bf),
                   jax.ShapeDtypeStruct((groups,TP,128),bf),jax.ShapeDtypeStruct((width,T),bf),jax.ShapeDtypeStruct((16,T),f32)),
        in_specs=[S]+[V]*7, out_specs=tuple([V]*6),
        scratch_shapes=[pltpu.VMEM((heads,48,TP),bf),pltpu.VMEM((groups,128,2*QT),bf)],
        compiler_params=pltpu.CompilerParams(vmem_limit_bytes=VM),
        cost_estimate=pl.CostEstimate(flops=12*10**9,bytes_accessed=10**7,transcendentals=5*10**6),
        name="attention_forward")(rng,n1,w,b,cos,sin,fq,fk)

def bwd_body(rng_ref,g_ref,n1_ref,wo_ref,w_ref,qt_ref,kt_ref,kp_ref,vn_ref,ot_ref,lse_ref,cos_ref,sin_ref,fq_ref,gin_ref,
             dw_ref,db_ref,gn_ref,dot_ref,delta_ref,dqt_ref,dkt_ref,dvt_ref,qbd_ref,dobd_ref):
    width=w_ref.shape[2]; heads=width//HD; groups=heads//2; T=n1_ref.shape[0]
    doT=dg(wo_ref[...],g_ref[...],0,1).astype(bf)
    dot_ref[...]=doT
    prod=doT.astype(f32)*ot_ref[...].astype(f32)
    for h in range(heads):
        delta_ref[h:h+1,:]=jnp.sum(prod[HD*h:HD*h+HD],axis=0,keepdims=True)
    dkt_ref[...]=jnp.zeros_like(dkt_ref); dvt_ref[...]=jnp.zeros_like(dvt_ref)
    z32=jnp.zeros((HD,QT),bf); z64=jnp.zeros((64,2*QT),bf)
    def qtile(i,_):
        q0=pl.multiple_of(i*QT,QT)
        lo=rng_ref[0,i]; n=rng_ref[1,i]
        fq=fq_ref[:,pl.ds(q0,QT)]
        for g in range(groups):
            q=qt_ref[64*g:64*g+64,pl.ds(q0,QT)]
            qbd_ref[g]=jnp.concatenate([jnp.concatenate([q[:HD],z32,fq],axis=0),jnp.concatenate([z32,q[HD:],fq],axis=0)],axis=1)
            d=dot_ref[64*g:64*g+64,pl.ds(q0,QT)]
            dobd_ref[g]=jnp.concatenate([jnp.concatenate([jnp.concatenate([d[:HD],z32],axis=0),jnp.concatenate([z32,d[HD:]],axis=0)],axis=1),z64],axis=0)
        def chunk(j,carry):
            k0=pl.multiple_of(lo*128+j*KC,128)
            new=[]
            for g in range(groups):
                s=jnp.dot(kp_ref[g,pl.ds(k0,KC),:],qbd_ref[g],preferred_element_type=f32)
                dp=jnp.dot(vn_ref[g,pl.ds(k0,KC),:],dobd_ref[g],preferred_element_type=f32)
                lse=jnp.concatenate([lse_ref[2*g:2*g+1,pl.ds(q0,QT)],lse_ref[2*g+1:2*g+2,pl.ds(q0,QT)]],axis=1)
                dl=jnp.concatenate([delta_ref[2*g:2*g+1,pl.ds(q0,QT)],delta_ref[2*g+1:2*g+2,pl.ds(q0,QT)]],axis=1)
                p=jnp.exp2(s-lse)
                ds=(p*(dp-dl)).astype(bf)
                p=p.astype(bf)
                dqs=[]
                for a in range(2):
                    h=2*g+a
                    rows=slice(HD*h,HD*h+HD); cols=slice(QT*a,QT*a+QT)
                    dvt_ref[rows,pl.ds(k0,KC)]+=dg(dot_ref[rows,pl.ds(q0,QT)],p[:,cols],1,1)
                    dkt_ref[rows,pl.ds(k0,KC)]+=dg(qt_ref[rows,pl.ds(q0,QT)],ds[:,cols],1,1)
                    dqs.append(carry[g][a]+jnp.dot(kt_ref[rows,pl.ds(k0,KC)],ds[:,cols],preferred_element_type=f32))
                new.append(tuple(dqs))
            return tuple(new)
        init=tuple((jnp.zeros((HD,QT),f32),)*2 for g in range(groups))
        res=lax.fori_loop(0,n,chunk,init)
        for g in range(groups):
            for a in range(2):
                h=2*g+a
                dqt_ref[HD*h:HD*h+HD,pl.ds(q0,QT)]=res[g][a]
        return 0
    lax.fori_loop(0,T//QT,qtile,0)
    cos=cos_ref[...]; sin=sin_ref[...]
    n1t=jnp.transpose(n1_ref[...])
    gt=jnp.transpose(g_ref[...])
    dw_ref[3]=dg(gt,ot_ref[...],1,1).astype(bf)
    gn=gin_ref[...]
    for c in range(3):
        if c==0: y=rope_rows(dqt_ref[...]*(HD**-0.5),cos,sin,heads,-1.0)
        elif c==1: y=rope_rows(dkt_ref[:,:T]*LN2,cos,sin,heads,-1.0)
        else: y=dvt_ref[:,:T]
        yb=y.astype(bf)
        db_ref[:,c:c+1]=jnp.sum(yb.astype(f32),axis=1,keepdims=True)
        dw_ref[c]=dg(n1t,yb,1,1).astype(bf)
        gn=gn+dg(yb,w_ref[c],0,1)
    gn_ref[...]=gn

def attn_bwd(rng,g,n1,wo,w,qt,kt,kp,vn,ot,lse,cos,sin,fq,gin):
    T=n1.shape[0]; width=w.shape[2]; D=n1.shape[1]; heads=width//HD; groups=heads//2; TP=T+128
    V=pl.BlockSpec(memory_space=pltpu.VMEM); S=pl.BlockSpec(memory_space=pltpu.SMEM)
    return pl.pallas_call(bwd_body,
        out_shape=(jax.ShapeDtypeStruct((4,D,width),bf),jax.ShapeDtypeStruct((width,8),f32),jax.ShapeDtypeStruct((T,D),f32)),
        in_specs=[S]+[V]*14, out_specs=tuple([V]*3),
        scratch_shapes=[pltpu.VMEM((width,T),bf),pltpu.VMEM((16,T),f32),pltpu.VMEM((width,T),f32),pltpu.VMEM((width,TP),f32),pltpu.VMEM((width,TP),f32),
                        pltpu.VMEM((groups,128,2*QT),bf),pltpu.VMEM((groups,128,2*QT),bf)],
        compiler_params=pltpu.CompilerParams(vmem_limit_bytes=VM),
        cost_estimate=pl.CostEstimate(flops=25*10**9,bytes_accessed=2*10**7,transcendentals=5*10**6),
        name="attention_backward")(rng,g,n1,wo,w,qt,kt,kp,vn,ot,lse,cos,sin,fq,gin)

def tables(seg):
    T=seg.shape[0]; TP=T+128
    ids=jnp.arange(8,dtype=jnp.int32)
    starts=jnp.sum((seg[None,:]<ids[:,None]).astype(jnp.int32),axis=1)
    ends=jnp.sum((seg[None,:]<=ids[:,None]).astype(jnp.int32),axis=1)
    onehot=(seg[None,:]==ids[:,None])
    before=jnp.sum(jnp.where(onehot,starts[:,None],0),axis=0)
    after=jnp.sum(jnp.where(onehot,ends[:,None],0),axis=0)
    pos=(jnp.arange(T,dtype=jnp.int32)-before).astype(f32)
    freq=10000.0**(-jnp.arange(0,HD,2).astype(f32)/HD)
    ang=freq[:,None]*pos[None,:]
    fq=jnp.where(onehot,0.0,-BIG).astype(bf)
    fq=jnp.concatenate([fq,jnp.zeros((56,T),bf)],axis=0)
    padk=jnp.broadcast_to((ids[:,None]==7),(8,TP-T))
    fk=jnp.concatenate([jnp.concatenate([onehot,padk],axis=1).astype(bf),jnp.zeros((56,TP),bf)],axis=0)
    lo=before[::QT]//128
    hi=after[QT-1::QT]
    n=(hi-lo*128+KC-1)//KC
    return jnp.cos(ang),jnp.sin(ang),fq,fk,jnp.stack([lo,n])

def ffn_body(oa_ref,ob_ref,woa_ref,wob_ref,x_ref,og_ref,nv_ref,hb_ref,w1a_ref,w1b_ref,w2a_ref,w2b_ref,
             out_ref,glow_ref,gres_ref,dw1_ref,dw2_ref,dhb_ref,vec_ref,
             res_ref,n2_ref,n2t_ref,ogt_ref,mix_ref,gn_ref):
    j=pl.program_id(0); half=pl.num_programs(0)//2; last=pl.num_programs(0)-1
    D=x_ref.shape[1]
    @pl.when(j==0)
    def _():
        att=dg(oa_ref[...],woa_ref[...],0,1)+dg(ob_ref[...],wob_ref[...],0,1)
        res=x_ref[...].astype(f32)+att+nv_ref[2:3]
        res_ref[...]=res
        cen=res-jnp.mean(res,axis=1,keepdims=True)
        var=jnp.mean(cen*cen,axis=1,keepdims=True)
        n2=cen*lax.rsqrt(var+EPS_NORM)*nv_ref[3:4]+nv_ref[4:5]
        n2b=n2.astype(bf)
        n2_ref[...]=n2b
        n2t_ref[...]=jnp.transpose(n2b)
        ogt_ref[...]=jnp.transpose(og_ref[...])
        mix_ref[...]=jnp.zeros_like(mix_ref)
        gn_ref[...]=jnp.zeros_like(gn_ref)
    own=j<half
    w1=jnp.where(own,w1a_ref[...],w1b_ref[...])
    w2=jnp.where(own,w2a_ref[...],w2b_ref[...])
    pre=jnp.dot(n2_ref[...],w1,preferred_element_type=f32)+hb_ref[0]
    gact=jnp.dot(og_ref[...],w2,preferred_element_type=f32)
    cdf=0.5+0.5*lax.erf(pre*(2.0**-0.5))
    act=(pre*cdf).astype(bf)
    pdf=jnp.exp(pre*pre*-0.5)*((2.0*math.pi)**-0.5)
    gpre=(gact*(cdf+pre*pdf)).astype(bf)
    mix_ref[...]+=dg(act,w2,1,1)
    gn_ref[...]+=dg(gpre,w1,1,1)
    dw1_ref[0]=jnp.dot(n2t_ref[...],gpre,preferred_element_type=f32).astype(bf)
    dw2_ref[0]=jnp.dot(ogt_ref[...],act,preferred_element_type=f32).astype(bf)
    dhb_ref[0]=jnp.sum(gpre.astype(f32),axis=0,keepdims=True)
    @pl.when(j==last)
    def _():
        res=res_ref[...]
        out_ref[...]=(res+mix_ref[...]+nv_ref[5:6]).astype(bf)
        og=og_ref[...].astype(f32)
        cen=res-jnp.mean(res,axis=1,keepdims=True)
        var=jnp.mean(cen*cen,axis=1,keepdims=True)
        r=lax.rsqrt(var+EPS_NORM)
        xh=cen*r
        gn=gn_ref[...]
        e=gn*nv_ref[3:4]
        gres=og+r*(e-jnp.mean(e,axis=1,keepdims=True)-xh*jnp.mean(e*xh,axis=1,keepdims=True))
        gres_ref[...]=gres
        glow_ref[...]=gres.astype(bf)
        vec_ref[...]=jnp.concatenate([jnp.sum(gres,axis=0,keepdims=True),jnp.sum(gn*xh,axis=0,keepdims=True),
            jnp.sum(gn,axis=0,keepdims=True),jnp.sum(og,axis=0,keepdims=True),jnp.zeros((4,D),f32)],axis=0)

def ffn(oa,ob,woa,wob,x,og,nv,hb,w1a,w1b,w2a,w2b):
    T,D=x.shape; F=w1a.shape[1]; FB=256; half=F//FB; nb=2*half
    V=pl.BlockSpec(memory_space=pltpu.VMEM)
    wa=pl.BlockSpec((D,FB),lambda j:(0,jnp.minimum(j,half-1)))
    wb=pl.BlockSpec((D,FB),lambda j:(0,jnp.maximum(j-half,0)))
    dw=pl.BlockSpec((1,D,FB),lambda j:(j//half,0,lax.rem(j,half)))
    bb=pl.BlockSpec((1,1,FB),lambda j:(j,0,0))
    return pl.pallas_call(ffn_body,grid=(nb,),
        out_shape=(jax.ShapeDtypeStruct((T,D),bf),jax.ShapeDtypeStruct((T,D),bf),jax.ShapeDtypeStruct((T,D),f32),
            jax.ShapeDtypeStruct((2,D,F),bf),jax.ShapeDtypeStruct((2,D,F),bf),jax.ShapeDtypeStruct((nb,1,FB),f32),jax.ShapeDtypeStruct((8,D),f32)),
        in_specs=[V]*7+[bb,wa,wb,wa,wb],out_specs=(V,V,V,dw,dw,bb,V),
        scratch_shapes=[pltpu.VMEM((T,D),f32),pltpu.VMEM((T,D),bf),pltpu.VMEM((D,T),bf),pltpu.VMEM((D,T),bf),pltpu.VMEM((T,D),f32),pltpu.VMEM((T,D),f32)],
        compiler_params=pltpu.CompilerParams(vmem_limit_bytes=VM),
        cost_estimate=pl.CostEstimate(flops=22*10**9,bytes_accessed=3*10**7,transcendentals=5*10**6),
        name="ffn")(oa,ob,woa,wob,x,og,nv,hb,w1a,w1b,w2a,w2b)

def tail_body(gn_ref,gres_ref,x_ref,nv_ref,out_ref,vec_ref):
    j=pl.program_id(0); D=x_ref.shape[1]
    x=x_ref[...].astype(f32)
    cen=x-jnp.mean(x,axis=1,keepdims=True)
    var=jnp.mean(cen*cen,axis=1,keepdims=True)
    r=lax.rsqrt(var+EPS_NORM)
    xh=cen*r
    gn=gn_ref[...]
    e=gn*nv_ref[0:1]
    out_ref[...]=(gres_ref[...]+r*(e-jnp.mean(e,axis=1,keepdims=True)-xh*jnp.mean(e*xh,axis=1,keepdims=True))).astype(bf)
    v=jnp.concatenate([jnp.sum(gn*xh,axis=0,keepdims=True),jnp.sum(gn,axis=0,keepdims=True),jnp.zeros((6,D),f32)],axis=0)
    @pl.when(j==0)
    def _(): vec_ref[...]=v
    @pl.when(j>0)
    def _(): vec_ref[...]+=v

def tail(gn,gres,x,nv):
    T,D=x.shape; B=256
    row=pl.BlockSpec((B,D),lambda j:(j,0)); one=pl.BlockSpec((8,D),lambda j:(0,0))
    return pl.pallas_call(tail_body,grid=(T//B,),out_shape=(jax.ShapeDtypeStruct((T,D),bf),jax.ShapeDtypeStruct((8,D),f32)),
        in_specs=[row,row,row,one],out_specs=(row,one),
        compiler_params=pltpu.CompilerParams(vmem_limit_bytes=VM),
        cost_estimate=pl.CostEstimate(flops=2*10**7,bytes_accessed=10**7,transcendentals=0),
        name="norm_backward")(gn,gres,x,nv)

def bit_groups(count):
    bits=count.bit_length()-1
    groups=[]
    top=bits
    while top>2:
        take=2 if top>3 else 1
        groups.append((top-take,take)); top-=take
    while top>0:
        groups.append((top-1,1)); top-=1
    return groups

def swap(value,axis_name,offset):
    n=lax.axis_size(axis_name)
    return lax.ppermute(value,axis_name,[(i,i^offset) for i in range(n)])

def order_blocks(blocks,place,axis):
    count=len(blocks)
    if count==1: return blocks[0]
    half=count//2
    low=place%half if half>1 else 0
    first=order_blocks(blocks[:half],low,axis); second=order_blocks(blocks[half:],low,axis)
    high=(place//half)%2
    return jnp.where(high==0,jnp.concatenate([first,second],axis),jnp.concatenate([second,first],axis))

def gather_step(value,group,axis):
    low,take=group
    place=(lax.axis_index("dp")>>low)%(1<<take)
    return order_blocks([value]+[swap(value,"dp",k<<low) for k in range(1,1<<take)],place,axis)

def scatter_step(value,group,axis,last_type):
    low,take=group
    place=(lax.axis_index("dp")>>low)%(1<<take)
    total=lax.dynamic_slice_in_dim(value,place,1,axis).astype(f32)
    for k in range(1,1<<take):
        total=total+swap(lax.dynamic_slice_in_dim(value,place^k,1,axis),"dp",k<<low).astype(f32)
    return total.astype(last_type)

def start_blocks(value,groups):
    return value.reshape((value.shape[0],)+(1,)*len(groups)+value.shape[1:])

def merge_blocks(value):
    return value.reshape((value.shape[0],-1,value.shape[-1]))

def gather_late(value,groups):
    value=start_blocks(value,groups)
    for at,group in enumerate(groups[:-1]): value=gather_step(value,group,1+at)
    peer=swap(value,"tp",1)
    at=len(groups)
    return merge_blocks(gather_step(value,groups[-1],at)),merge_blocks(gather_step(peer,groups[-1],at))

def gather_early(value,groups):
    value=start_blocks(jnp.stack([value,swap(value,"tp",1)]).reshape((-1,)+value.shape[1:]),groups)
    for at,group in enumerate(groups): value=gather_step(value,group,1+at)
    value=merge_blocks(value)
    half=value.shape[0]//2
    return value[:half],value[half:]

def scatter(value,groups,shard_rows):
    shape=(value.shape[0],)+tuple(1<<take for _,take in groups)+(shard_rows,value.shape[-1])
    value=value.reshape(shape)
    for at in range(len(groups)-1,-1,-1):
        value=scatter_step(value,groups[at],1+at,bf)
    return value.reshape((shape[0],shard_rows,shape[-1]))

def sum_all(value):
    value=value+swap(value,"tp",1)
    step=1
    while step<lax.axis_size("dp"):
        value=value+swap(value,"dp",step); step*=2
    return value

def by_peer(own,peer,axis):
    mine=lax.axis_index("tp")
    return jnp.where(mine==0,jnp.concatenate([own,peer],axis),jnp.concatenate([peer,own],axis))

def lamb_moments(weight, gradient, moment_one, moment_two):
    first_new = BETA_ONE * moment_one + (1.0 - BETA_ONE) * gradient
    second_new = BETA_TWO * moment_two + (1.0 - BETA_TWO) * gradient * gradient
    corrected = first_new / (1.0 - BETA_ONE**STEP)
    variance = second_new / (1.0 - BETA_TWO**STEP)
    update = corrected / (jnp.sqrt(variance) + EPS_ADAM) + DECAY * weight
    return (first_new, second_new, update)

def sum_squares(array):
    return jnp.sum(array * array, axis=tuple(range(1, array.ndim)))

def on_device(inputs,out_grad,segment_ids,attn_weights,ffn_weights,head_bias,hidden_bias,norm_vectors,
    attn_first,ffn_first,head_first,hidden_first,vector_first,attn_second,ffn_second,head_second,hidden_second,vector_second):
    dpn=lax.axis_size("dp"); tpn=lax.axis_size("tp"); mine=lax.axis_index("tp")
    rows,slots=segment_ids.shape
    assert rows==tpn==2
    groups=bit_groups(dpn)
    shard=attn_weights.shape[1]; hw=attn_weights.shape[2]; fw=ffn_weights.shape[2]; D=inputs.shape[1]
    qkv_own,qkv_peer=gather_late(attn_weights[:3].astype(bf),groups)
    wo_own,wo_peer=gather_late(attn_weights[3:].astype(bf),groups)
    w1_own,w1_peer=gather_late(ffn_weights[:1].astype(bf),groups)
    w2_own,w2_peer=gather_early(ffn_weights[1:].astype(bf),groups)
    bias_own=jnp.concatenate([head_bias.reshape(-1),hidden_bias])
    bias_peer=swap(bias_own.reshape(-1,hw),"tp",1).reshape(-1)
    def split_bias(b):
        hb=jnp.concatenate([b[:3*hw].reshape(3,hw),jnp.zeros((5,hw),f32)],0).T
        return hb,b[3*hw:]
    hb_own,hid_own=split_bias(bias_own); hb_peer,hid_peer=split_bias(bias_peer)
    x=lax.dynamic_slice_in_dim(inputs,mine*slots,slots,0)
    og=lax.dynamic_slice_in_dim(out_grad,mine*slots,slots,0)
    seg=lax.dynamic_index_in_dim(segment_ids,mine,0,keepdims=False)
    cos,sin,fq,fk,rng=tables(seg)
    nv=jnp.concatenate([norm_vectors,jnp.zeros((2,D),f32)],0)
    xf=x.astype(f32)
    cen=xf-jnp.mean(xf,axis=1,keepdims=True)
    var=jnp.mean(cen*cen,axis=1,keepdims=True)
    n1=(cen*lax.rsqrt(var+EPS_NORM)*norm_vectors[0]+norm_vectors[1]).astype(bf)
    fwd_own=attn_fwd(rng,n1,qkv_own,hb_own,cos,sin,fq,fk)
    fwd_peer=attn_fwd(rng,n1,qkv_peer,hb_peer,cos,sin,fq,fk)
    hid=jnp.concatenate([hid_own,hid_peer]).reshape(-1,1,256)
    out_low,glow,gres,dw1,dw2,dhb,vec2=ffn(fwd_own[4],fwd_peer[4],wo_own[0],wo_peer[0],x,og,nv,hid,w1_own[0],w1_peer[0],w2_own[0],w2_peer[0])
    layer_output=by_peer(out_low,swap(out_low,"tp",1),0)
    gffn=scatter(jnp.concatenate([dw1,dw2],0) if False else jnp.stack([dw1[0],dw2[0],dw1[1],dw2[1]]),groups,shard)
    gffn=gffn[:2].astype(f32)+swap(gffn[2:],"tp",1).astype(f32)
    def back(fwd,wo,w,gin):
        return attn_bwd(rng,glow,n1,wo[0],w,fwd[0],fwd[1],fwd[2],fwd[3],fwd[4],fwd[5],cos,sin,fq,gin)
    dwp,dbp,gn=back(fwd_peer,wo_peer,qkv_peer,jnp.zeros((slots,D),f32))
    gpeer=scatter(dwp,groups,shard)
    gpeer_in=swap(gpeer,"tp",1)
    dwo,dbo,gn=back(fwd_own,wo_own,qkv_own,gn)
    gattn=scatter(dwo,groups,shard).astype(f32)+gpeer_in.astype(f32)
    in_low,vec1=tail(gn,gres,x,nv)
    input_grad=by_peer(in_low,swap(in_low,"tp",1),0)
    head_full=by_peer(dbo[:,:3].T,dbp[:,:3].T,1)
    half_hidden=dhb.reshape(2,-1)
    hidden_full=by_peer(half_hidden[0],half_hidden[1],0)
    small=jnp.concatenate([head_full,vec1[:2],vec2[0:4],hidden_full.reshape(-1,D)],0)
    small=sum_all(small)
    sum_head=lax.dynamic_slice_in_dim(small[:3],mine*hw,hw,1)
    sum_vectors=small[3:9]
    sum_hidden=lax.dynamic_slice_in_dim(small[9:].reshape(-1),mine*fw,fw,0)
    masters=[attn_weights,ffn_weights,head_bias,hidden_bias.reshape(1,-1),norm_vectors]
    replicas=[1.0,1.0,1.0/dpn,1.0/dpn,1.0/(dpn*tpn)]
    grads=[gattn,gffn,sum_head,sum_hidden.reshape(1,-1),sum_vectors]
    firsts=[attn_first,ffn_first,head_first,hidden_first.reshape(1,-1),vector_first]
    seconds=[attn_second,ffn_second,head_second,hidden_second.reshape(1,-1),vector_second]
    results=[lamb_moments(masters[i],grads[i],firsts[i],seconds[i]) for i in range(5)]
    wterms=jnp.concatenate([sum_squares(masters[i])*replicas[i] for i in range(5)])
    uterms=jnp.concatenate([sum_squares(results[i][2])*replicas[i] for i in range(5)])
    terms=jnp.stack([wterms,uterms])
    norms=jnp.sqrt(sum_all(jnp.pad(terms,((0,6),(0,112)))))[:2,:16]
    ratio=norms[0]/norms[1]
    counts=[4,2,3,1,6]
    new=[]
    at=0
    for i in range(5):
        piece=ratio[at:at+counts[i]].reshape((-1,)+(1,)*(masters[i].ndim-1))
        new.append(masters[i]-RATE*piece*results[i][2]); at+=counts[i]
    return (layer_output,input_grad,new[0],new[1],new[2],new[3].reshape(-1),new[4],
        results[0][0],results[1][0],results[2][0],results[3][0].reshape(-1),results[4][0],
        results[0][1][:3],results[0][1][3],results[1][1],results[2][1],results[3][1].reshape(-1),results[4][1][2:],results[4][1][:2],norms)


def solution(mesh):
    in_specs = (
        P("dp", None),
        P("dp", None),
        P("dp", None),
        P(None, "dp", "tp"),
        P(None, "dp", "tp"),
        P(None, "tp"),
        P("tp"),
        P(),
        P(None, "dp", "tp"),
        P(None, "dp", "tp"),
        P(None, "tp"),
        P("tp"),
        P(),
        P(None, "dp", "tp"),
        P(None, "dp", "tp"),
        P(None, "tp"),
        P("tp"),
        P(),
    )
    out_specs = (
        P("dp", None),
        P("dp", None),
        P(None, "dp", "tp"),
        P(None, "dp", "tp"),
        P(None, "tp"),
        P("tp"),
        P(),
        P(None, "dp", "tp"),
        P(None, "dp", "tp"),
        P(None, "tp"),
        P("tp"),
        P(),
        P(None, "dp", "tp"),
        P("dp", "tp"),
        P(None, "dp", "tp"),
        P(None, "tp"),
        P("tp"),
        P(),
        P(),
        P(),
    )
    return jax.shard_map(
        on_device, mesh=mesh, in_specs=in_specs, out_specs=out_specs, check_vma=False
    )
```

time: 1320 us -> 519 us (0.39)
  waiting for transfers between devices: 522 us -> 140 us
  matrix products: 279 us -> 0 us
  Pallas kernels: 0 us -> 181 us
  local copies, waits for them, and re-layouts: 218 us -> 41.2 us
  other arithmetic: 167 us -> 45.7 us
  blocking collectives: 99.6 us -> 0 us
  starting transfers between devices: 0.25 us -> 99.6 us
    psum x4 -> x0, waiting for transfers between devices: 440 us -> none  [the longest x1 181 us: on_device(): lax.psum((grad_attn, grad_ffn, grad_head_bias, grad_hidden_bias, grad_vec...]
    dot_general x40 -> x0, matrix products: 279 us -> none  [the longest x4 60.6 us: attend_block_back(): jnp.einsum('qhd,khd->hqk', grad_heads, values_row, preferred_element_type...]
    pallas_call x0 -> x6, Pallas kernels: none -> 181 us  [the longest x2 75.1 us: attn_bwd(): pl.pallas_call(bwd_body, out_shape=(jax.ShapeDtypeStruct((4, D, width), b...]
    ppermute x0 -> x57, waiting for transfers between devices: none -> 140 us  [swap(): return lax.ppermute(value, axis_name, [(i, i ^ offset) for i in range(n)])]
    ppermute x0 -> x57, starting transfers between devices: none -> 99.6 us  [swap(): return lax.ppermute(value, axis_name, [(i, i ^ offset) for i in range(n)])]
    psum x2 -> x0, blocking collectives: 99.6 us -> none  [the longest x1 62.5 us: on_device(): lax.psum((grad_attn, grad_ffn, grad_head_bias, grad_hidden_bias, grad_vec...]
    while x64 -> x0, local copies, waits for them, and re-layouts: 84.5 us -> none
    all_gather x2 -> x0, waiting for transfers between devices: 81.5 us -> none  [the longest x1 44.8 us: on_device(): lax.all_gather(ffn_weights.astype(jnp.bfloat16), 'dp', axis=1, tiled=True)]
  transfers between devices with their start and end apart: 6 -> 57, of which waited for: 6 -> 21; matrix products, arithmetic and copies ran while one was open for 4% -> 14% of each run, Pallas kernels for 0% -> 27%
where the time goes in v1:
time: 519 us; the launch traced here: 511 us
  Pallas kernels  181 us (35%)
  waiting for transfers between devices  140 us (27%)
  starting transfers between devices  99.6 us (19%)
  other arithmetic  45.7 us (9%)
  local copies, waits for them, and re-layouts  41.2 us (8%)
    ppermute x57, waiting for transfers between devices, swap(): return lax.ppermute(value, axis_name, [(i, i ^ offset) for i in range(n)])  140 us
    ppermute x57, starting transfers between devices, swap(): return lax.ppermute(value, axis_name, [(i, i ^ offset) for i in range(n)])  99.6 us
    pallas_call x2, Pallas kernels, attn_bwd(): pl.pallas_call(bwd_body, out_shape=(jax.ShapeDtypeStruct((4, D, width), b...  75.1 us
    pallas_call x2, Pallas kernels, attn_fwd(): pl.pallas_call(fwd_body, out_shape=(jax.ShapeDtypeStruct((width, T), bf),...  59.2 us
    pallas_call x1, Pallas kernels, ffn(): pl.pallas_call(ffn_body, grid=(nb,), out_shape=(jax.ShapeDtypeStruct((T,...  40.6 us
  transfers between devices with their start and end apart: 57, of which 21 were waited for; matrix products, arithmetic and copies ran while one was open for 14% of the time, Pallas kernels for 27%

profile of v1, /device:TPU:0, one launch (start us, length us, event | category | flops | bytes accessed | tf_op | source)
XLA Modules:
  0.0 511.2 jit_solution(13302691029428492649)
XLA Ops:
  2.6 4.0 collective-permute-start.16
  37.3 3.3 collective-permute-start.2
  55.0 6.0 %collective-permute-done.24 = bf16[2,1,1,1,40,1280]{5,4,0,3,2,1:T(8,128)(2,1)S(1)} collective-permute-done((bf16[2,1,1,1,40,1280]{5,4,0,3,2,1:T(8,128)(2,1)S(1)}, bf16[2,1,1,1,40,1280]{5,4,0,3,2,1:T(8,128)(2,1)S(1)}, u32[]{:S(2)}, u32[]{:S(2)}) %collective-permute-start.24) | collective-permute-done | bytes 204832 | tf_op jit(solution)/shard_map/ppermute | solution.py:313
  72.6 11.4 %collective-permute-done.5 = bf16[3,4,2,1,40,320]{5,4,0,1,3,2:T(8,128)(2,1)S(1)} collective-permute-done((bf16[3,4,2,1,40,320]{5,4,0,1,3,2:T(8,128)(2,1)S(1)}, bf16[3,4,2,1,40,320]{5,4,0,1,3,2:T(8,128)(2,1)S(1)}, u32[]{:S(2)}, u32[]{:S(2)}) %collective-permute-start.5) | collective-permute-done | bytes 614432 | tf_op jit(solution)/shard_map/ppermute | solution.py:313
  84.0 29.8 %attention_forward.2 = (bf16[320,1024]{1,0:T(8,128)(2,1)}, bf16[320,1152]{1,0:T(8,128)(2,1)}, bf16[5,1152,128]{2,1,0:T(8,128)(2,1)}, bf16[5,1152,128]{2,1,0:T(8,...) custom-call(s32[2,8]{1,0:T(2,128)} %pad_add_fusion.1.rng_ref, bf16[1024,640]{1,0:T(8,128)(2,1)} %fusion.5.n1_ref, ...), custom_call_target="tpu_custom_call" | custom-call | flops 12000000000 | bytes 10000000 | tf_op jit(solution)/shard_map/attention_forward/pallas_call | solution.py:106
  118.0 29.4 %attention_forward.3 = (bf16[320,1024]{1,0:T(8,128)(2,1)}, bf16[320,1152]{1,0:T(8,128)(2,1)}, bf16[5,1152,128]{2,1,0:T(8,128)(2,1)}, bf16[5,1152,128]{2,1,0:T(8,...) custom-call(s32[2,8]{1,0:T(2,128)} %pad_add_fusion.1.rng_ref, bf16[1024,640]{1,0:T(8,128)(2,1)} %fusion.5.n1_ref, ...), custom_call_target="tpu_custom_call" | custom-call | flops 12000000000 | bytes 10000000 | tf_op jit(solution)/shard_map/attention_forward/pallas_call | solution.py:106
  152.3 40.6 %ffn.1 = (bf16[1024,640]{1,0:T(8,128)(2,1)}, bf16[1024,640]{1,0:T(8,128)(2,1)}, f32[1024,640]{1,0:T(8,128)}, bf16[2,640,1280]{2,1,0:T(8,128)(2,1)}, bf16[2,640,1...) custom-call(bf16[320,1024]{1,0:T(8,128)(2,1)} %get-tuple-element.47.oa_ref.ot_ref, ...), custom_call_target="tpu_custom_call" | custom-call | flops 22000001024 | bytes 30000000 | tf_op jit(solution)/shard_map/ffn/pallas_call | solution.py:266
  192.8 3.3 fusion.43
  201.7 37.7 %attention_backward.2 = (bf16[4,640,320]{2,1,0:T(8,128)(2,1)}, f32[320,8]{1,0:T(8,128)}, f32[1024,640]{1,0:T(8,128)}) custom-call(s32[2,8]{1,0:T(2,128)} %pad_add_fusion.1.rng_ref, bf16[1024,640]{1,0:T(8,128)(2,1)} %get-tuple-element.50.g_ref, bf16[1024,640]{1,0:T(8,128)(2,1)} %fusion.5.n1_ref, bf16[640,320]{1,0:T(8,128)(2,1)} %bitcast.141, ...), custom_call_target="tpu_custom_call" | custom-call | flops 24999999488 | bytes 20000000 | tf_op jit(solution)/shard_map/attention_backward/pallas_call | solution.py:180
  239.3 37.5 %attention_backward.3 = (bf16[4,640,320]{2,1,0:T(8,128)(2,1)}, f32[320,8]{1,0:T(8,128)}, f32[1024,640]{1,0:T(8,128)}) custom-call(s32[2,8]{1,0:T(2,128)} %pad_add_fusion.1.rng_ref, bf16[1024,640]{1,0:T(8,128)(2,1)} %get-tuple-element.50.g_ref, bf16[1024,640]{1,0:T(8,128)(2,1)} %fusion.5.n1_ref, bf16[640,320]{1,0:T(8,128)(2,1)} %bitcast.139, ...), custom_call_target="tpu_custom_call" | custom-call | flops 24999999488 | bytes 20000000 | tf_op jit(solution)/shard_map/attention_backward/pallas_call | solution.py:180
  279.0 5.7 %norm_backward.1 = (bf16[1024,640]{1,0:T(8,128)(2,1)}, f32[8,640]{1,0:T(8,128)}) custom-call(f32[1024,640]{1,0:T(8,128)} %get-tuple-element.62.gn_ref, f32[1024,640]{1,0:T(8,128)} %get-tuple-element.63.gres_ref, bf16[1024,640]{1,0:T(8,128)(2,1)} %copy-done.2, f32[8,640]{1,0:T(8,128)} %concatenate.1006.nv_ref), custom_call_target="tpu_custom_call" | custom-call | flops 20000000 | bytes 10000000 | tf_op jit(solution)/shard_map/norm_backward/pallas_call | solution.py:294
  285.7 3.8 collective-permute-done.47
  291.1 3.7 collective-permute-done.49
  294.9 10.7 %collective-permute-start.50 = (f32[13,640]{1,0:T(8,128)S(1)}, f32[13,640]{1,0:T(8,128)S(1)}, u32[]{:S(2)}, u32[]{:S(2)}) collective-permute-start(f32[13,640]{1,0:T(8,128)S(1)} %add.375), channel_id=1, source_target_pairs={{0,8},{2,10},{4,12},{6,14},{8,0},{10,2},{12,4},{14,6},{16,24},{18,... | collective-permute-start | bytes 99848 | tf_op jit(solution)/shard_map/ppermute | solution.py:313
  307.6 19.3 %collective-permute-start.51 = (f32[13,640]{1,0:T(8,128)S(1)}, f32[13,640]{1,0:T(8,128)S(1)}, u32[]{:S(2)}, u32[]{:S(2)}) collective-permute-start(f32[13,640]{1,0:T(8,128)S(1)} %add.376), channel_id=1, source_target_pairs={{0,16},{2,18},{4,20},{6,22},{8,24},{10,26},{12,28},{14,30},{16,0},... | collective-permute-start | bytes 99848 | tf_op jit(solution)/shard_map/ppermute | solution.py:313
  326.9 3.8 constant_dynamic-slice_fusion.12
  349.0 40.8 %collective-permute-done.36 = bf16[4,4,1,1,40,320]{5,4,0,3,2,1:T(8,128)(2,1)S(1)} collective-permute-done((bf16[4,4,1,1,40,320]{5,4,0,3,2,1:T(8,128)(2,1)S(1)}, bf16[4,4,1,1,40,320]{5,4,0,3,2,1:T(8,128)(2,1)S(1)}, u32[]{:S(2)}, u32[]{:S(2)}) %collective-permute-start.36) | collective-permute-done | bytes 409632 | tf_op jit(solution)/shard_map/ppermute | solution.py:313
  395.6 4.1 collective-permute-done.31
  406.8 19.3 %collective-permute-done.39 = bf16[4,1,1,1,40,320]{5,4,0,3,2,1:T(8,128)(2,1)S(1)} collective-permute-done((bf16[4,1,1,1,40,320]{5,4,0,3,2,1:T(8,128)(2,1)S(1)}, bf16[4,1,1,1,40,320]{5,4,0,3,2,1:T(8,128)(2,1)S(1)}, u32[]{:S(2)}, u32[]{:S(2)}) %collective-permute-start.39) | collective-permute-done | bytes 102432 | tf_op jit(solution)/shard_map/ppermute | solution.py:313
  426.1 13.6 %collective-permute-start.32 = (bf16[4,1,1,1,40,320]{5,4,0,3,2,1:T(8,128)(2,1)S(1)}, bf16[4,1,1,1,40,320]{5,4,0,3,2,1:T(8,128)(2,1)S(1)}, u32[]{:S(2)}, u32[]{:S(2)}) collective-permute-start(bf16[4,1,1,1,40,320]{5,4,0,3,2,1:T(8,128)(2,1)S(1)} %get-tuple-element.121), channel_id=1, source_target_pairs={{0,8},{2,10},{4,12},{6,14},{8,0},{10,2},{12,4},{14,6},{16,24},{18,... | collective-permute-start | bytes 307208 | tf_op jit(solution)/shard_map/ppermute | solution.py:313
  444.7 5.8 %collective-permute-done.33 = bf16[4,1,1,1,40,320]{5,4,0,3,2,1:T(8,128)(2,1)S(1)} collective-permute-done((bf16[4,1,1,1,40,320]{5,4,0,3,2,1:T(8,128)(2,1)S(1)}, bf16[4,1,1,1,40,320]{5,4,0,3,2,1:T(8,128)(2,1)S(1)}, u32[]{:S(2)}, u32[]{:S(2)}) %collective-permute-start.33) | collective-permute-done | bytes 102432 | tf_op jit(solution)/shard_map/ppermute | solution.py:313
  452.9 25.3 %collective-permute-done.46 = bf16[2,40,1280]{2,1,0:T(8,128)(2,1)S(1)} collective-permute-done((bf16[2,40,1280]{2,1,0:T(8,128)(2,1)S(1)}, bf16[2,40,1280]{2,1,0:T(8,128)(2,1)S(1)}, u32[]{:S(2)}, u32[]{:S(2)}) %collective-permute-start.46) | collective-permute-done | bytes 204832 | tf_op jit(solution)/shard_map/ppermute | solution.py:313
  491.5 3.8 maximum_select_fusion.2
  496.3 4.0 maximum_select_fusion.1
  (326 shorter events, 140.3 us)
Async XLA Ops:
  2.6 44.9 %collective-permute-start.16 = (bf16[1,1,1,1,40,1280]{5,4,3,2,1,0:T(8,128)(2,1)}, bf16[1,1,1,1,40,1280]{5,4,3,2,1,0:T(8,128)(2,1)}, u32[]{:S(2)}, u32[]{:S(2)}) collective-permute-start(bf16[1,1,1,1,40,1280]{5,4,3,2,1,0:T(8,128)(2,1)} %get-tuple-element.132), channel_id=1, source_target_pairs={{0,16},{2,18},{4,20},{6,22},{8,24},{10,26},{12,28},{14,30},{16,0},... | collective-permute-start | bytes 307208 | tf_op jit(solution)/shard_map/ppermute | solution.py:313
  6.6 41.0 %collective-permute-start.17 = (bf16[1,1,1,1,40,1280]{5,4,3,2,1,0:T(8,128)(2,1)}, bf16[1,1,1,1,40,1280]{5,4,3,2,1,0:T(8,128)(2,1)}, u32[]{:S(2)}, u32[]{:S(2)}) collective-permute-start(bf16[1,1,1,1,40,1280]{5,4,3,2,1,0:T(8,128)(2,1)} %get-tuple-element.132), channel_id=1, source_target_pairs={{0,24},{2,26},{4,28},{6,30},{8,16},{10,18},{12,20},{14,22},{16,8},... | collective-permute-start | bytes 307208 | tf_op jit(solution)/shard_map/ppermute | solution.py:313
  8.0 43.6 %collective-permute-start.15 = (bf16[1,1,1,1,40,1280]{5,4,3,2,1,0:T(8,128)(2,1)}, bf16[1,1,1,1,40,1280]{5,4,3,2,1,0:T(8,128)(2,1)}, u32[]{:S(2)}, u32[]{:S(2)}) collective-permute-start(bf16[1,1,1,1,40,1280]{5,4,3,2,1,0:T(8,128)(2,1)} %get-tuple-element.132), channel_id=1, source_target_pairs={{0,8},{2,10},{4,12},{6,14},{8,0},{10,2},{12,4},{14,6},{16,24},{18,... | collective-permute-start | bytes 307208 | tf_op jit(solution)/shard_map/ppermute | solution.py:313
  9.8 20.0 %collective-permute-start.9 = (bf16[1,1,1,1,40,320]{5,4,3,2,1,0:T(8,128)(2,1)}, bf16[1,1,1,1,40,320]{5,4,3,2,1,0:T(8,128)(2,1)}, u32[]{:S(2)}, u32[]{:S(2)}) collective-permute-start(bf16[1,1,1,1,40,320]{5,4,3,2,1,0:T(8,128)(2,1)} %get-tuple-element.144), channel_id=1, source_target_pairs={{0,16},{2,18},{4,20},{6,22},{8,24},{10,26},{12,28},{14,30},{16,0},... | collective-permute-start | bytes 76808 | tf_op jit(solution)/shard_map/ppermute | solution.py:313
  61.8 52.0 %collective-permute-start.26 = (bf16[2,4,1,1,40,1280]{5,4,1,0,3,2:T(8,128)(2,1)S(1)}, bf16[2,4,1,1,40,1280]{5,4,1,0,3,2:T(8,128)(2,1)S(1)}, u32[]{:S(2)}, u32[]{:S(2)}) collective-permute-start(bf16[2,4,1,1,40,1280]{5,4,1,0,3,2:T(8,128)(2,1)S(1)} %maximum_select_fusion.10), channel_id=1, source_target_pairs={{0,4},{2,6},{4,0},{6,2},{8,12},{10,14},{12,8},{14,10},{16,20},{18,... | collective-permute-start | bytes 2457608 | tf_op jit(solution)/shard_map/ppermute | solution.py:313
  63.2 20.7 %collective-permute-start.5 = (bf16[3,4,2,1,40,320]{5,4,0,1,3,2:T(8,128)(2,1)S(1)}, bf16[3,4,2,1,40,320]{5,4,0,1,3,2:T(8,128)(2,1)S(1)}, u32[]{:S(2)}, u32[]{:S(2)}) collective-permute-start(bf16[3,4,2,1,40,320]{5,4,0,1,3,2:T(8,128)(2,1)S(1)} %maximum_select_fusion.11), channel_id=1, source_target_pairs={{0,1},{1,0},{2,3},{3,2},{4,5},{5,4},{6,7},{7,6},{8,9},{9,8},{10,11... | collective-permute-start | bytes 1843208 | tf_op jit(solution)/shard_map/ppermute | solution.py:313
  68.3 47.9 %collective-permute-start.20 = (bf16[1,4,2,1,40,1280]{5,4,1,3,2,0:T(8,128)(2,1)S(1)}, bf16[1,4,2,1,40,1280]{5,4,1,3,2,0:T(8,128)(2,1)S(1)}, u32[]{:S(2)}, u32[]{:S(2)}) collective-permute-start(bf16[1,4,2,1,40,1280]{5,4,1,3,2,0:T(8,128)(2,1)S(1)} %maximum_select_fusion.8), channel_id=1, source_target_pairs={{0,1},{1,0},{2,3},{3,2},{4,5},{5,4},{6,7},{7,6},{8,9},{9,8},{10,11... | collective-permute-start | bytes 2457608 | tf_op jit(solution)/shard_map/ppermute | solution.py:313
  69.7 45.0 %collective-permute-start.19 = (bf16[1,4,2,1,40,1280]{5,4,1,3,2,0:T(8,128)(2,1)S(1)}, bf16[1,4,2,1,40,1280]{5,4,1,3,2,0:T(8,128)(2,1)S(1)}, u32[]{:S(2)}, u32[]{:S(2)}) collective-permute-start(bf16[1,4,2,1,40,1280]{5,4,1,3,2,0:T(8,128)(2,1)S(1)} %maximum_select_fusion.8), channel_id=1, source_target_pairs={{0,2},{2,0},{4,6},{6,4},{8,10},{10,8},{12,14},{14,12},{16,18},{18,... | collective-permute-start | bytes 2457608 | tf_op jit(solution)/shard_map/ppermute | solution.py:313
  84.0 32.2 %collective-permute-start.6 = (bf16[3,4,2,1,40,320]{5,4,0,1,3,2:T(8,128)(2,1)S(1)}, bf16[3,4,2,1,40,320]{5,4,0,1,3,2:T(8,128)(2,1)S(1)}, u32[]{:S(2)}, u32[]{:S(2)}) collective-permute-start(bf16[3,4,2,1,40,320]{5,4,0,1,3,2:T(8,128)(2,1)S(1)} %collective-permute-done.5), channel_id=1, source_target_pairs={{0,2},{2,0},{4,6},{6,4},{8,10},{10,8},{12,14},{14,12},{16,18},{18,... | collective-permute-start | bytes 1843208 | tf_op jit(solution)/shard_map/ppermute | solution.py:313
  114.1 34.9 %collective-permute-start.27 = (bf16[2,4,2,1,40,1280]{5,4,1,0,3,2:T(8,128)(2,1)S(1)}, bf16[2,4,2,1,40,1280]{5,4,1,0,3,2:T(8,128)(2,1)S(1)}, u32[]{:S(2)}, u32[]{:S(2)}) collective-permute-start(bf16[2,4,2,1,40,1280]{5,4,1,0,3,2:T(8,128)(2,1)S(1)} %maximum_select_fusion.5), channel_id=1, source_target_pairs={{0,2},{2,0},{4,6},{6,4},{8,10},{10,8},{12,14},{14,12},{16,18},{18,... | collective-permute-start | bytes 4915208 | tf_op jit(solution)/shard_map/ppermute | solution.py:313
  116.2 31.2 %collective-permute-start.21 = (bf16[1,4,2,1,40,1280]{5,4,1,3,2,0:T(8,128)(2,1)S(1)}, bf16[1,4,2,1,40,1280]{5,4,1,3,2,0:T(8,128)(2,1)S(1)}, u32[]{:S(2)}, u32[]{:S(2)}) collective-permute-start(bf16[1,4,2,1,40,1280]{5,4,1,3,2,0:T(8,128)(2,1)S(1)} %collective-permute-done.20), channel_id=1, source_target_pairs={{0,2},{2,0},{4,6},{6,4},{8,10},{10,8},{12,14},{14,12},{16,18},{18,... | collective-permute-start | bytes 2457608 | tf_op jit(solution)/shard_map/ppermute | solution.py:313
  199.5 138.2 %collective-permute-start.41 = (bf16[4,4,2,1,40,1280]{5,4,0,3,2,1:T(8,128)(2,1)}, bf16[4,4,2,1,40,1280]{5,4,0,3,2,1:T(8,128)(2,1)}, u32[]{:S(2)}, u32[]{:S(2)}) collective-permute-start(bf16[4,4,2,1,40,1280]{5,4,0,3,2,1:T(8,128)(2,1)} %copy.108), channel_id=1, source_target_pairs={{0,2},{2,0},{4,6},{6,4},{8,10},{10,8},{12,14},{14,12},{16,18},{18,... | collective-permute-start | bytes 9830408 | tf_op jit(solution)/shard_map/ppermute | solution.py:313
  307.6 25.8 %collective-permute-start.51 = (f32[13,640]{1,0:T(8,128)S(1)}, f32[13,640]{1,0:T(8,128)S(1)}, u32[]{:S(2)}, u32[]{:S(2)}) collective-permute-start(f32[13,640]{1,0:T(8,128)S(1)} %add.376), channel_id=1, source_target_pairs={{0,16},{2,18},{4,20},{6,22},{8,24},{10,26},{12,28},{14,30},{16,0},... | collective-permute-start | bytes 99848 | tf_op jit(solution)/shard_map/ppermute | solution.py:313
  340.6 51.1 %collective-permute-start.42 = (bf16[4,4,1,1,40,1280]{5,4,0,3,2,1:T(8,128)(2,1)S(1)}, bf16[4,4,1,1,40,1280]{5,4,0,3,2,1:T(8,128)(2,1)S(1)}, u32[]{:S(2)}, u32[]{:S(2)}) collective-permute-start(bf16[4,4,1,1,40,1280]{5,4,0,3,2,1:T(8,128)(2,1)S(1)} %constant_dynamic-slice_fusion.4), channel_id=1, source_target_pairs={{0,4},{2,6},{4,0},{6,2},{8,12},{10,14},{12,8},{14,10},{16,20},{18,... | collective-permute-start | bytes 4915208 | tf_op jit(solution)/shard_map/ppermute | solution.py:313
  345.3 44.5 %collective-permute-start.36 = (bf16[4,4,1,1,40,320]{5,4,0,3,2,1:T(8,128)(2,1)S(1)}, bf16[4,4,1,1,40,320]{5,4,0,3,2,1:T(8,128)(2,1)S(1)}, u32[]{:S(2)}, u32[]{:S(2)}) collective-permute-start(bf16[4,4,1,1,40,320]{5,4,0,3,2,1:T(8,128)(2,1)S(1)} %constant_dynamic-slice_fusion.10), channel_id=1, source_target_pairs={{0,4},{2,6},{4,0},{6,2},{8,12},{10,14},{12,8},{14,10},{16,20},{18,... | collective-permute-start | bytes 1228808 | tf_op jit(solution)/shard_map/ppermute | solution.py:313
  347.0 52.8 %collective-permute-start.31 = (bf16[4,4,1,1,40,320]{5,4,0,3,2,1:T(8,128)(2,1)S(1)}, bf16[4,4,1,1,40,320]{5,4,0,3,2,1:T(8,128)(2,1)S(1)}, u32[]{:S(2)}, u32[]{:S(2)}) collective-permute-start(bf16[4,4,1,1,40,320]{5,4,0,3,2,1:T(8,128)(2,1)S(1)} %constant_dynamic-slice_fusion.16), channel_id=1, source_target_pairs={{0,4},{2,6},{4,0},{6,2},{8,12},{10,14},{12,8},{14,10},{16,20},{18,... | collective-permute-start | bytes 1228808 | tf_op jit(solution)/shard_map/ppermute | solution.py:313
  392.2 47.6 %collective-permute-start.43 = (bf16[4,1,1,1,40,1280]{5,4,0,3,2,1:T(8,128)(2,1)S(1)}, bf16[4,1,1,1,40,1280]{5,4,0,3,2,1:T(8,128)(2,1)S(1)}, u32[]{:S(2)}, u32[]{:S(2)}) collective-permute-start(bf16[4,1,1,1,40,1280]{5,4,0,3,2,1:T(8,128)(2,1)S(1)} %get-tuple-element.116), channel_id=1, source_target_pairs={{0,8},{2,10},{4,12},{6,14},{8,0},{10,2},{12,4},{14,6},{16,24},{18,... | collective-permute-start | bytes 1228808 | tf_op jit(solution)/shard_map/ppermute | solution.py:313
  392.7 47.1 %collective-permute-start.44 = (bf16[4,1,1,1,40,1280]{5,4,0,3,2,1:T(8,128)(2,1)S(1)}, bf16[4,1,1,1,40,1280]{5,4,0,3,2,1:T(8,128)(2,1)S(1)}, u32[]{:S(2)}, u32[]{:S(2)}) collective-permute-start(bf16[4,1,1,1,40,1280]{5,4,0,3,2,1:T(8,128)(2,1)S(1)} %get-tuple-element.118), channel_id=1, source_target_pairs={{0,16},{2,18},{4,20},{6,22},{8,24},{10,26},{12,28},{14,30},{16,0},... | collective-permute-start | bytes 1228808 | tf_op jit(solution)/shard_map/ppermute | solution.py:313
  399.7 42.6 %collective-permute-start.45 = (bf16[4,1,1,1,40,1280]{5,4,0,3,2,1:T(8,128)(2,1)S(1)}, bf16[4,1,1,1,40,1280]{5,4,0,3,2,1:T(8,128)(2,1)S(1)}, u32[]{:S(2)}, u32[]{:S(2)}) collective-permute-start(bf16[4,1,1,1,40,1280]{5,4,0,3,2,1:T(8,128)(2,1)S(1)} %get-tuple-element.117), channel_id=1, source_target_pairs={{0,24},{2,26},{4,28},{6,30},{8,16},{10,18},{12,20},{14,22},{16,8},... | collective-permute-start | bytes 1228808 | tf_op jit(solution)/shard_map/ppermute | solution.py:313
  400.8 25.3 %collective-permute-start.39 = (bf16[4,1,1,1,40,320]{5,4,0,3,2,1:T(8,128)(2,1)S(1)}, bf16[4,1,1,1,40,320]{5,4,0,3,2,1:T(8,128)(2,1)S(1)}, u32[]{:S(2)}, u32[]{:S(2)}) collective-permute-start(bf16[4,1,1,1,40,320]{5,4,0,3,2,1:T(8,128)(2,1)S(1)} %get-tuple-element.125), channel_id=1, source_target_pairs={{0,24},{2,26},{4,28},{6,30},{8,16},{10,18},{12,20},{14,22},{16,8},... | collective-permute-start | bytes 307208 | tf_op jit(solution)/shard_map/ppermute | solution.py:313
  403.9 87.6 %collective-permute-start.29 = (bf16[1024,640]{1,0:T(8,128)(2,1)S(1)}, bf16[1024,640]{1,0:T(8,128)(2,1)}, u32[]{:S(2)}, u32[]{:S(2)}) collective-permute-start(bf16[1024,640]{1,0:T(8,128)(2,1)S(1)} %copy-done.11), channel_id=1, source_target_pairs={{0,1},{1,0},{2,3},{3,2},{4,5},{5,4},{6,7},{7,6},{8,9},{9,8},{10,11... | collective-permute-start | bytes 3932168 | tf_op jit(solution)/shard_map/ppermute | solution.py:313
  426.1 17.4 %collective-permute-start.32 = (bf16[4,1,1,1,40,320]{5,4,0,3,2,1:T(8,128)(2,1)S(1)}, bf16[4,1,1,1,40,320]{5,4,0,3,2,1:T(8,128)(2,1)S(1)}, u32[]{:S(2)}, u32[]{:S(2)}) collective-permute-start(bf16[4,1,1,1,40,320]{5,4,0,3,2,1:T(8,128)(2,1)S(1)} %get-tuple-element.121), channel_id=1, source_target_pairs={{0,8},{2,10},{4,12},{6,14},{8,0},{10,2},{12,4},{14,6},{16,24},{18,... | collective-permute-start | bytes 307208 | tf_op jit(solution)/shard_map/ppermute | solution.py:313
  443.6 52.7 %collective-permute-start.28 = (bf16[1024,640]{1,0:T(8,128)(2,1)S(1)}, bf16[1024,640]{1,0:T(8,128)(2,1)}, u32[]{:S(2)}, u32[]{:S(2)}) collective-permute-start(bf16[1024,640]{1,0:T(8,128)(2,1)S(1)} %copy-done.9), channel_id=1, source_target_pairs={{0,1},{1,0},{2,3},{3,2},{4,5},{5,4},{6,7},{7,6},{8,9},{9,8},{10,11... | collective-permute-start | bytes 3932168 | tf_op jit(solution)/shard_map/ppermute | solution.py:313
  450.4 27.8 %collective-permute-start.46 = (bf16[2,40,1280]{2,1,0:T(8,128)(2,1)S(1)}, bf16[2,40,1280]{2,1,0:T(8,128)(2,1)S(1)}, u32[]{:S(2)}, u32[]{:S(2)}) collective-permute-start(bf16[2,40,1280]{2,1,0:T(8,128)(2,1)S(1)} %slice_bitcast_fusion), channel_id=1, source_target_pairs={{0,1},{1,0},{2,3},{3,2},{4,5},{5,4},{6,7},{7,6},{8,9},{9,8},{10,11... | collective-permute-start | bytes 614408 | tf_op jit(solution)/shard_map/ppermute | solution.py:313
  (70 other events, 889.0 us)
